TPU v7x, 32 devices: a whole 2x2x4 slice. The times are simulated.
32 devices in a mesh: dom: 8 (over z, x), tp: 4 (over y, core).
Axes of the slice: x: 2, y: 2, z: 4, core: 2. Of those that a mesh axis runs over, the one named last changes fastest.
Arguments:
- features: bfloat16 [32768, 512], P('dom'), may hold values from -6 to 6
- adjacency: bfloat16 [32768, 128], P('dom'), may hold values from -0.5 to 0.5
- node_mask: int32 [32768], P('dom'), may hold values 0 or 1
- mask_token: bfloat16 [512], replicated, may hold values from -6 to 6
- enc_weight: bfloat16 [512, 512], P(None, 'tp'), may hold values from -0.25 to 0.25
- enc_bias: bfloat16 [512], P('tp'), may hold values from -3 to 3
- gain: float32 [512], replicated, may hold values from -0.25 to 0.25
- requests: int32 [8, 8], P(None, 'dom'), may hold values from 0 to 31
- pair_first: int32 [8, 4, 64], P('dom', 'tp'), may hold values from 0 to 7
- pair_second: int32 [8, 4, 64], P('dom', 'tp'), may hold values from 0 to 9
- label_words: int32 [8, 4, 64, 8, 128], P('dom', 'tp'), may hold values from 0 to 65280
- pair_count: int32 [8, 4], P('dom', 'tp'), may hold values from 16 to 64, as said below
Outputs:
- weight_grad: float32 [512, 512], P(None, 'tp')
- bias_grad: float32 [512], P('tp')
- gain_grad: float32 [512], P('tp')
Inputs may be any that keep to these rules, and one draw needn't show every extreme that they name: Every partition requests exactly one block from every partition, itself included. Slots p >= pair_count are padding; some device has all 64 slots live.
All inputs are finite; a program needn't handle non-finite values. No bound on the sum of `node_mask` on one device may be relied on, other than what follows from the above.
Results may differ from a plain program's by a relative error of at most 0.0018.
Values may be sent and summed in bfloat16 or wider, within the bound.
A program may use at most 128 MiB of HBM per device.

v0:
```python
import jax
import jax.numpy as jnp
from jax import lax
from jax.sharding import PartitionSpec as P

GROUP = 8


LOSS_NORM = 256.0


def silu_slope(value):
    sig = jax.nn.sigmoid(value)
    return sig * (1.0 + value * (1.0 - sig))


def unpack_labels(words):
    shifts = jnp.arange(16, dtype=jnp.int32)
    bits = jnp.bitwise_and(jnp.right_shift(words[:, :, None, :], shifts[None, None, :, None]), 1)
    return bits.reshape(words.shape[0], words.shape[1] * 16, words.shape[2]).astype(jnp.float32)


def decode(stack, local_count, first, second, words, count, gain):
    total = stack.shape[0]
    first_acc = jnp.zeros((local_count, stack.shape[1], stack.shape[2]), jnp.float32)
    second_acc = jnp.zeros((total, stack.shape[1], stack.shape[2]), jnp.float32)

    def step(carry, group):
        first_acc, second_acc = carry
        start = group * GROUP
        index_a = lax.dynamic_slice_in_dim(first, start, GROUP, 0)
        index_b = lax.dynamic_slice_in_dim(second, start, GROUP, 0)
        word_rows = lax.dynamic_slice_in_dim(words, start, GROUP, 0)
        tile_a = stack[index_a]
        tile_b = stack[index_b]
        scaled = (tile_a * gain[None, None, :]).astype(jnp.bfloat16)
        logits = jnp.einsum("pif,pjf->pij", scaled, tile_b, preferred_element_type=jnp.float32)
        live = (start + jnp.arange(GROUP, dtype=jnp.int32) < count).astype(jnp.float32)
        slope = (
            (jax.nn.sigmoid(logits) - unpack_labels(word_rows)) * live[:, None, None] / LOSS_NORM
        ).astype(jnp.bfloat16)
        part_a = jnp.einsum("pij,pjf->pif", slope, tile_b, preferred_element_type=jnp.float32)
        part_b = jnp.einsum("pij,pif->pjf", slope, scaled, preferred_element_type=jnp.float32)
        return ((first_acc.at[index_a].add(part_a), second_acc.at[index_b].add(part_b)), None)

    groups = jnp.arange(first.shape[0] // GROUP, dtype=jnp.int32)
    (first_acc, second_acc), _ = lax.scan(step, (first_acc, second_acc), groups)
    return (first_acc, second_acc)


def body(
    features,
    adjacency,
    node_mask,
    mask_token,
    enc_weight,
    enc_bias,
    gain,
    requests,
    pair_first,
    pair_second,
    label_words,
    pair_count,
):
    nodes, width = features.shape
    block = adjacency.shape[1]
    nblocks = nodes // block
    quarter = enc_weight.shape[1]
    masked = jnp.where(node_mask[:, None] == 1, mask_token[None, :], features)
    blocks = masked.reshape(nblocks, block, width)
    mixed = jnp.einsum(
        "bij,bjf->bif",
        adjacency.reshape(nblocks, block, block),
        blocks,
        preferred_element_type=jnp.float32,
    )
    agg = (blocks.astype(jnp.float32) + mixed).reshape(nodes, width).astype(jnp.bfloat16)
    pre = jnp.dot(agg, enc_weight, preferred_element_type=jnp.float32) + enc_bias.astype(
        jnp.float32
    )
    z_own = jax.nn.silu(pre).astype(jnp.bfloat16).reshape(nblocks, block, quarter)
    lanes = lax.axis_size("tp")
    own_count = nblocks // lanes
    whole = lax.all_gather(z_own, "tp", axis=2, tiled=True)
    local = lax.dynamic_slice_in_dim(whole, lax.axis_index("tp") * own_count, own_count, 0)
    wanted = requests[:, 0]
    outgoing = z_own[wanted]
    remote = lax.all_to_all(
        lax.all_to_all(outgoing, "dom", split_axis=0, concat_axis=0, tiled=True),
        "tp",
        split_axis=0,
        concat_axis=2,
        tiled=True,
    )
    stack = jnp.concatenate([local, remote], axis=0)
    first_acc, second_acc = decode(
        stack,
        own_count,
        pair_first[0, 0],
        pair_second[0, 0],
        label_words[0, 0],
        pair_count[0, 0],
        gain,
    )
    local_grad = gain[None, None, :] * first_acc + second_acc[:own_count]
    gain_part = jnp.sum(local.astype(jnp.float32) * first_acc, axis=1, keepdims=True)
    own_local, own_gain = (
        lax.all_to_all(local_grad, "tp", split_axis=2, concat_axis=0, tiled=True),
        lax.all_to_all(gain_part, "tp", split_axis=2, concat_axis=0, tiled=True),
    )
    returned = lax.all_to_all(
        lax.all_to_all(
            second_acc[own_count:].astype(jnp.bfloat16),
            "tp",
            split_axis=2,
            concat_axis=0,
            tiled=True,
        ),
        "dom",
        split_axis=0,
        concat_axis=0,
        tiled=True,
    ).astype(jnp.float32)
    chooser = (wanted[:, None] == jnp.arange(nblocks, dtype=jnp.int32)[None, :]).astype(jnp.float32)
    own_grad = own_local + jnp.einsum(
        "rn,rif->nif", chooser, returned, precision=lax.Precision.HIGHEST
    )
    dpre = own_grad.reshape(nodes, quarter) * silu_slope(pre)
    weight_part = lax.dot_general(
        agg, dpre.astype(jnp.bfloat16), (((0,), (0,)), ((), ())), preferred_element_type=jnp.float32
    )
    bias_part = jnp.sum(dpre, axis=0)
    gain_sum = jnp.sum(own_gain, axis=(0, 1))
    weight_grad, bias_grad, gain_grad = lax.psum((weight_part, bias_part, gain_sum), "dom")
    return (weight_grad, bias_grad, gain_grad)


def solution(mesh):
    placed = (
        P("dom", None),
        P("dom", None),
        P("dom"),
        P(),
        P(None, "tp"),
        P("tp"),
        P(),
        P(None, "dom"),
        P("dom", "tp", None),
        P("dom", "tp", None),
        P("dom", "tp", None, None, None),
        P("dom", "tp"),
    )
    return jax.shard_map(
        body,
        mesh=mesh,
        in_specs=placed,
        out_specs=(P(None, "tp"), P("tp"), P("tp")),
        check_vma=False,
    )
```

profile of v0, /device:TPU:0, one launch (start us, length us, event | category | flops | bytes accessed | tf_op | source)
XLA Modules:
  0.0 387.6 jit_solution(1374723033368995257)
XLA Ops:
  8.7 2.6 broadcast_select_fusion
  12.6 3.0 multiply_convert_fusion.3
  17.5 16.1 %all_to_all.73 = bf16[8,128,128]{2,1,0:T(8,128)(2,1)} all-to-all(bf16[8,128,128]{2,1,0:T(8,128)(2,1)S(1)} %gather_fusion.2), channel_id=1, replica_groups=mesh['dom'=8,'tp'=4] {'dom'}, dimensions={0} | all-to-all | bytes 524288 | tf_op jit(solution)/shard_map/all_to_all | solution.py:89
  33.6 3.4 all-to-all-start.1
  37.0 9.1 %all-to-all-done.1 = bf16[8,128,128]{2,1,0:T(8,128)(2,1)S(1)} async-done(((bf16[8,128,128]{2,1,0:T(8,128)(2,1)}), bf16[8,128,128]{2,1,0:T(8,128)(2,1)S(1)}, u32[]{:S(2)}, u32[]{:S(2)}) %all-to-all-start.1) | async-done | bytes 262176 | tf_op jit(solution)/shard_map/all_to_all | solution.py:88
  46.5 9.9 %all-gather.2.cloned.1.call-done = bf16[32,128,512]{2,1,0:T(8,128)(2,1)} async-done(((bf16[32,128,128]{2,1,0:T(8,128)(2,1)}), bf16[32,128,512]{2,1,0:T(8,128)(2,1)}) %all-gather.2.cloned.1.call-update) | async-done | bytes 4194320 | tf_op jit(solution)/shard_map/all_gather | solution.py:84
  62.4 173.2 %while.12 = (s32[]{:T(128)}, f32[8,128,512]{2,1,0:T(8,128)}, f32[10,128,512]{2,1,0:T(8,128)}, s32[8]{0:T(128)S(1)}, s32[64]{0:T(128)S(1)}, /*index=5*/bf16[10,12...) while((s32[]{:T(128)}, f32[8,128,512]{2,1,0:T(8,128)}, ...), condition=%wide.region_3.4_spmd, body=%wide.region_0.3_spmd.sunk | while | flops 408160352 | bytes 35502768 | solution.py:47
  67.5 2.3 gather_fusion.1
  73.9 4.2 %scatter_fusion = f32[8,128,512]{2,1,0:T(8,128)} fusion(f32[8,128,512]{2,1,0:T(8,128)} %get-tuple-element.171, s32[8]{0:T(128)S(1)} %get-tuple-element.153, f32[8,128,512]{2,1,0:T(8,128)S(1)} %fusion.44), kind=kCustom, calls=%fused_computation.3.clone.1 | custom fusion | flops 524288 | bytes 6291488 | tf_op jit(solution)/shard_map/while/body/eval_jaxpr/scatter-add | solution.py:44
  79.8 4.2 %scatter_fusion.1 = f32[10,128,512]{2,1,0:T(8,128)} fusion(f32[10,128,512]{2,1,0:T(8,128)} %get-tuple-element.172, s32[8]{0:T(128)S(1)} %get-tuple-element.154, f32[8,128,512]{2,1,0:T(8,128)S(1)} %fusion.45), kind=kCustom, calls=%fused_computation.4.clone.1 | custom fusion | flops 524288 | bytes 6291488 | tf_op jit(solution)/shard_map/while/body/eval_jaxpr/scatter-add | solution.py:44
  89.1 2.3 gather_fusion.1
  95.5 4.0 %scatter_fusion = f32[8,128,512]{2,1,0:T(8,128)} fusion(f32[8,128,512]{2,1,0:T(8,128)} %get-tuple-element.171, s32[8]{0:T(128)S(1)} %get-tuple-element.153, f32[8,128,512]{2,1,0:T(8,128)S(1)} %fusion.44), kind=kCustom, calls=%fused_computation.3.clone.1 | custom fusion | flops 524288 | bytes 6291488 | tf_op jit(solution)/shard_map/while/body/eval_jaxpr/scatter-add | solution.py:44
  101.3 4.2 %scatter_fusion.1 = f32[10,128,512]{2,1,0:T(8,128)} fusion(f32[10,128,512]{2,1,0:T(8,128)} %get-tuple-element.172, s32[8]{0:T(128)S(1)} %get-tuple-element.154, f32[8,128,512]{2,1,0:T(8,128)S(1)} %fusion.45), kind=kCustom, calls=%fused_computation.4.clone.1 | custom fusion | flops 524288 | bytes 6291488 | tf_op jit(solution)/shard_map/while/body/eval_jaxpr/scatter-add | solution.py:44
  108.6 1.9 gather_fusion
  110.5 2.3 gather_fusion.1
  117.0 4.1 %scatter_fusion = f32[8,128,512]{2,1,0:T(8,128)} fusion(f32[8,128,512]{2,1,0:T(8,128)} %get-tuple-element.171, s32[8]{0:T(128)S(1)} %get-tuple-element.153, f32[8,128,512]{2,1,0:T(8,128)S(1)} %fusion.44), kind=kCustom, calls=%fused_computation.3.clone.1 | custom fusion | flops 524288 | bytes 6291488 | tf_op jit(solution)/shard_map/while/body/eval_jaxpr/scatter-add | solution.py:44
  122.8 4.2 %scatter_fusion.1 = f32[10,128,512]{2,1,0:T(8,128)} fusion(f32[10,128,512]{2,1,0:T(8,128)} %get-tuple-element.172, s32[8]{0:T(128)S(1)} %get-tuple-element.154, f32[8,128,512]{2,1,0:T(8,128)S(1)} %fusion.45), kind=kCustom, calls=%fused_computation.4.clone.1 | custom fusion | flops 524288 | bytes 6291488 | tf_op jit(solution)/shard_map/while/body/eval_jaxpr/scatter-add | solution.py:44
  132.1 2.3 gather_fusion.1
  138.5 4.3 %scatter_fusion = f32[8,128,512]{2,1,0:T(8,128)} fusion(f32[8,128,512]{2,1,0:T(8,128)} %get-tuple-element.171, s32[8]{0:T(128)S(1)} %get-tuple-element.153, f32[8,128,512]{2,1,0:T(8,128)S(1)} %fusion.44), kind=kCustom, calls=%fused_computation.3.clone.1 | custom fusion | flops 524288 | bytes 6291488 | tf_op jit(solution)/shard_map/while/body/eval_jaxpr/scatter-add | solution.py:44
  144.6 4.3 %scatter_fusion.1 = f32[10,128,512]{2,1,0:T(8,128)} fusion(f32[10,128,512]{2,1,0:T(8,128)} %get-tuple-element.172, s32[8]{0:T(128)S(1)} %get-tuple-element.154, f32[8,128,512]{2,1,0:T(8,128)S(1)} %fusion.45), kind=kCustom, calls=%fused_computation.4.clone.1 | custom fusion | flops 524288 | bytes 6291488 | tf_op jit(solution)/shard_map/while/body/eval_jaxpr/scatter-add | solution.py:44
  152.0 1.9 gather_fusion
  153.9 2.3 gather_fusion.1
  160.4 4.2 %scatter_fusion = f32[8,128,512]{2,1,0:T(8,128)} fusion(f32[8,128,512]{2,1,0:T(8,128)} %get-tuple-element.171, s32[8]{0:T(128)S(1)} %get-tuple-element.153, f32[8,128,512]{2,1,0:T(8,128)S(1)} %fusion.44), kind=kCustom, calls=%fused_computation.3.clone.1 | custom fusion | flops 524288 | bytes 6291488 | tf_op jit(solution)/shard_map/while/body/eval_jaxpr/scatter-add | solution.py:44
  166.3 4.3 %scatter_fusion.1 = f32[10,128,512]{2,1,0:T(8,128)} fusion(f32[10,128,512]{2,1,0:T(8,128)} %get-tuple-element.172, s32[8]{0:T(128)S(1)} %get-tuple-element.154, f32[8,128,512]{2,1,0:T(8,128)S(1)} %fusion.45), kind=kCustom, calls=%fused_computation.4.clone.1 | custom fusion | flops 524288 | bytes 6291488 | tf_op jit(solution)/shard_map/while/body/eval_jaxpr/scatter-add | solution.py:44
  173.7 1.9 gather_fusion
  175.6 2.3 gather_fusion.1
  182.1 4.1 %scatter_fusion = f32[8,128,512]{2,1,0:T(8,128)} fusion(f32[8,128,512]{2,1,0:T(8,128)} %get-tuple-element.171, s32[8]{0:T(128)S(1)} %get-tuple-element.153, f32[8,128,512]{2,1,0:T(8,128)S(1)} %fusion.44), kind=kCustom, calls=%fused_computation.3.clone.1 | custom fusion | flops 524288 | bytes 6291488 | tf_op jit(solution)/shard_map/while/body/eval_jaxpr/scatter-add | solution.py:44
  187.9 4.2 %scatter_fusion.1 = f32[10,128,512]{2,1,0:T(8,128)} fusion(f32[10,128,512]{2,1,0:T(8,128)} %get-tuple-element.172, s32[8]{0:T(128)S(1)} %get-tuple-element.154, f32[8,128,512]{2,1,0:T(8,128)S(1)} %fusion.45), kind=kCustom, calls=%fused_computation.4.clone.1 | custom fusion | flops 524288 | bytes 6291488 | tf_op jit(solution)/shard_map/while/body/eval_jaxpr/scatter-add | solution.py:44
  197.2 2.3 gather_fusion.1
  203.7 4.2 %scatter_fusion = f32[8,128,512]{2,1,0:T(8,128)} fusion(f32[8,128,512]{2,1,0:T(8,128)} %get-tuple-element.171, s32[8]{0:T(128)S(1)} %get-tuple-element.153, f32[8,128,512]{2,1,0:T(8,128)S(1)} %fusion.44), kind=kCustom, calls=%fused_computation.3.clone.1 | custom fusion | flops 524288 | bytes 6291488 | tf_op jit(solution)/shard_map/while/body/eval_jaxpr/scatter-add | solution.py:44
  209.5 4.3 %scatter_fusion.1 = f32[10,128,512]{2,1,0:T(8,128)} fusion(f32[10,128,512]{2,1,0:T(8,128)} %get-tuple-element.172, s32[8]{0:T(128)S(1)} %get-tuple-element.154, f32[8,128,512]{2,1,0:T(8,128)S(1)} %fusion.45), kind=kCustom, calls=%fused_computation.4.clone.1 | custom fusion | flops 524288 | bytes 6291488 | tf_op jit(solution)/shard_map/while/body/eval_jaxpr/scatter-add | solution.py:44
  217.0 1.9 gather_fusion
  218.9 2.3 gather_fusion.1
  225.4 4.2 %scatter_fusion = f32[8,128,512]{2,1,0:T(8,128)} fusion(f32[8,128,512]{2,1,0:T(8,128)} %get-tuple-element.171, s32[8]{0:T(128)S(1)} %get-tuple-element.153, f32[8,128,512]{2,1,0:T(8,128)S(1)} %fusion.44), kind=kCustom, calls=%fused_computation.3.clone.1 | custom fusion | flops 524288 | bytes 6291488 | tf_op jit(solution)/shard_map/while/body/eval_jaxpr/scatter-add | solution.py:44
  231.3 4.2 %scatter_fusion.1 = f32[10,128,512]{2,1,0:T(8,128)} fusion(f32[10,128,512]{2,1,0:T(8,128)} %get-tuple-element.172, s32[8]{0:T(128)S(1)} %get-tuple-element.154, f32[8,128,512]{2,1,0:T(8,128)S(1)} %fusion.45), kind=kCustom, calls=%fused_computation.4.clone.1 | custom fusion | flops 524288 | bytes 6291488 | tf_op jit(solution)/shard_map/while/body/eval_jaxpr/scatter-add | solution.py:44
  235.5 5.2 %copy.52 = f32[10,128,512]{1,0,2:T(8,128)} copy(f32[10,128,512]{2,1,0:T(8,128)} %get-tuple-element.57) | data formatting | bytes 5242880 | tf_op jit(solution)/shard_map/while | solution.py:47
  244.6 3.4 all-to-all-start.3
  248.0 4.0 %slice_add_fusion = f32[8,128,512]{1,0,2:T(8,128)} fusion(f32[10,128,512]{1,0,2:T(8,128)} %copy.52, f32[8,128,512]{1,0,2:T(8,128)} %copy.51, f32[512]{0:T(512)S(1)} %get-tuple-element.218), kind=kLoop, calls=%fused_computation.29 | loop fusion | flops 1048576 | bytes 6293504 | tf_op jit(solution)/shard_map/add | solution.py:105
  252.0 2.0 all-to-all-done.3
  254.0 4.5 %all-to-all-start.2 = ((f32[8,128,512]{1,0,2:T(8,128)}), f32[8,128,512]{1,0,2:T(8,128)}, u32[]{:S(2)}, u32[]{:S(2)}) async-start(f32[8,128,512]{1,0,2:T(8,128)} %slice_add_fusion), calls=%async_computation.2 | async-start | bytes 4194304 | tf_op jit(solution)/shard_map/all_to_all | solution.py:108
  259.3 24.9 %all-to-all-done.2 = f32[8,128,512]{1,0,2:T(8,128)} async-done(((f32[8,128,512]{1,0,2:T(8,128)}), f32[8,128,512]{1,0,2:T(8,128)}, u32[]{:S(2)}, u32[]{:S(2)}) %all-to-all-start.2) | async-done | bytes 2097184 | tf_op jit(solution)/shard_map/all_to_all | solution.py:108
  284.2 5.7 %all-to-all-start.4 = ((bf16[8,128,128]{2,1,0:T(8,128)(2,1)}), bf16[8,128,128]{2,1,0:T(8,128)(2,1)S(1)}, u32[]{:S(2)}, u32[]{:S(2)}) async-start(bf16[8,128,128]{2,1,0:T(8,128)(2,1)} %bitcast.77), calls=%async_computation.4 | async-start | bytes 524288 | tf_op jit(solution)/shard_map/all_to_all | solution.py:111
  294.2 2.4 copy.53
  296.7 2.0 all-to-all-done.4
  298.7 3.4 all-to-all-start.5
  306.5 2.0 fusion.11
  310.7 20.4 %all-reduce = (f32[128]{0:T(128)}, f32[128]{0:T(128)}) all-reduce(f32[128]{0:T(128)S(1)} %get-tuple-element.80, f32[128]{0:T(128)S(1)} %bitcast_reduce_fusion), channel_id=1, replica_groups=mesh['dom'=8,'tp'=4] {'dom'}, use_global_device_ids=true, to_apply=%region_6.7 | all-reduce | flops 256 | bytes 2048 | tf_op jit(solution)/shard_map/psum | solution.py:134
  331.1 48.0 %all-reduce.3.cloned.1.call-done = f32[512,128]{1,0:T(8,128)} async-done(((f32[512,128]{1,0:T(8,128)}), f32[512,128]{1,0:T(8,128)}) %all-reduce.3.cloned.1.call-update) | async-done | bytes 262160 | tf_op jit(solution)/shard_map/psum | solution.py:134
  (187 shorter events, 102.0 us)
Async XLA Ops:
  7.2 4.1 %copy-start = (bf16[4096,128]{1,0:T(8,128)(2,1)S(1)}, bf16[4096,128]{1,0:T(8,128)(2,1)}, u32[]{:S(2)}) copy-start(bf16[4096,128]{1,0:T(8,128)(2,1)} %param.15) | copy-start | bytes 3145732
  7.2 49.2 %all-gather.2.cloned.1.call-start = ((), (), s32[]{:S(2)}) async-start(), calls=%async_computation.6 | async-start | bytes 5242880 | tf_op jit(solution)/shard_map/all_gather | solution.py:84
  11.3 1.3 copy-start.11
  12.6 3.1 copy-start.4
  12.6 3.1 copy-start.10
  33.6 12.5 %all-to-all-start.1 = ((bf16[8,128,128]{2,1,0:T(8,128)(2,1)}), bf16[8,128,128]{2,1,0:T(8,128)(2,1)S(1)}, u32[]{:S(2)}, u32[]{:S(2)}) async-start(bf16[8,128,128]{2,1,0:T(8,128)(2,1)} %all_to_all.73), calls=%async_computation.1 | async-start | bytes 524288 | tf_op jit(solution)/shard_map/all_to_all | solution.py:88
  58.9 3.4 copy-start.7
  59.0 3.4 copy-start.8
  59.0 3.4 copy-start.9
  67.4 3.0 copy-start.3
  69.8 1.0 copy-start.2
  89.1 3.0 copy-start.3
  91.4 1.0 copy-start.2
  110.5 3.0 copy-start.3
  112.8 1.0 copy-start.2
  132.0 3.0 copy-start.3
  134.4 1.0 copy-start.2
  153.9 3.0 copy-start.3
  156.2 1.0 copy-start.2
  175.6 3.0 copy-start.3
  177.9 1.0 copy-start.2
  197.2 3.0 copy-start.3
  199.5 1.0 copy-start.2
  218.9 3.0 copy-start.3
  221.2 1.0 copy-start.2
  235.5 6.3 %copy-start.1 = (f32[8,128,512]{2,1,0:T(8,128)S(1)}, f32[8,128,512]{2,1,0:T(8,128)}, u32[]{:S(2)}) copy-start(f32[8,128,512]{2,1,0:T(8,128)} %get-tuple-element.56) | copy-start | bytes 6291460
  244.6 9.4 %all-to-all-start.3 = ((bf16[2,128,512]{1,0,2:T(2,128)(2,1)}), bf16[2,128,512]{1,0,2:T(2,128)(2,1)S(1)}, u32[]{:S(2)}, u32[]{:S(2)}) async-start(bf16[2,128,512]{1,0,2:T(2,128)(2,1)} %copy.54), calls=%async_computation.3 | async-start | bytes 524288 | tf_op jit(solution)/shard_map/all_to_all | solution.py:112
  254.0 30.2 %all-to-all-start.2 = ((f32[8,128,512]{1,0,2:T(8,128)}), f32[8,128,512]{1,0,2:T(8,128)}, u32[]{:S(2)}, u32[]{:S(2)}) async-start(f32[8,128,512]{1,0,2:T(8,128)} %slice_add_fusion), calls=%async_computation.2 | async-start | bytes 4194304 | tf_op jit(solution)/shard_map/all_to_all | solution.py:108
  284.2 14.4 %all-to-all-start.4 = ((bf16[8,128,128]{2,1,0:T(8,128)(2,1)}), bf16[8,128,128]{2,1,0:T(8,128)(2,1)S(1)}, u32[]{:S(2)}, u32[]{:S(2)}) async-start(bf16[8,128,128]{2,1,0:T(8,128)(2,1)} %bitcast.77), calls=%async_computation.4 | async-start | bytes 524288 | tf_op jit(solution)/shard_map/all_to_all | solution.py:111
  298.7 9.8 %all-to-all-start.5 = ((f32[4,1,1024]{2,1,0:T(1,128)}), f32[4,1,1024]{2,1,0:T(1,128)S(1)}, u32[]{:S(2)}, u32[]{:S(2)}) async-start(f32[4,1,1024]{2,1,0:T(1,128)} %reshape.90), calls=%async_computation.5 | async-start | bytes 32768 | tf_op jit(solution)/shard_map/all_to_all | solution.py:109
  302.1 77.0 %all-reduce.3.cloned.1.call-start = ((), (), s32[]{:S(2)}) async-start(), calls=%async_computation.7 | async-start | bytes 524288 | tf_op jit(solution)/shard_map/psum | solution.py:134
  302.7 1.6 copy-start.6
  304.3 2.2 copy-start.5
Sparse Core Ops, SparseCore 0:
  15.8 40.5 all-gather.1
  308.6 70.4 all-reduce.2
where the time goes:
time: 391 us; the launch traced here: 388 us
  waiting for transfers between devices  96 us (25%)
  other arithmetic  95.6 us (24%)
  local copies, waits for them, and re-layouts  73.2 us (19%)
  matrix products  45.7 us (12%)
  blocking collectives  36.4 us (9%)
  starting transfers between devices  20.5 us (5%)
  between operations  14.3 us (4%)
  loops' own time  5.86 us (1%)
    psum x1, waiting for transfers between devices, body(): lax.psum((weight_part, bias_part, gain_sum), 'dom')  48 us
    scatter-add x8, other arithmetic, step(): second_acc.at[index_b].add(part_b)  33.9 us
    scatter-add x8, other arithmetic, step(): first_acc.at[index_a].add(part_a)  33.4 us
    all_to_all x1, waiting for transfers between devices, body(): lax.all_to_all(local_grad, 'tp', split_axis=2, concat_axis=0, tiled=True)  24.9 us
    psum x1, blocking collectives, body(): lax.psum((weight_part, bias_part, gain_sum), 'dom')  20.4 us
    gather x8, local copies, waits for them, and re-layouts, step(): tile_a = stack[index_a]  18.4 us
    all_to_all x1, blocking collectives, body(): lax.all_to_all(outgoing, 'dom', split_axis=0, concat_axis=0, tiled=True)  16.1 us
    gather x8, local copies, waits for them, and re-layouts, step(): tile_b = stack[index_b]  15.4 us
  transfers between devices with their start and end apart: 7, of which 6 were waited for; matrix products, arithmetic and copies ran while one was open for 5% of the time, Pallas kernels for 0%

commit v1 on v0

v1 whole, which is shorter than its diff:
```python
import functools

import jax
import jax.numpy as jnp
from jax import lax
from jax.experimental import pallas as pl
from jax.experimental.pallas import tpu as pltpu
from jax.sharding import PartitionSpec as P

UNROLL = 4
INV_NORM = 1.0 / 256.0
MESH = pl.DeviceIdType.MESH
VMEM_LIMIT = 32 * 1024 * 1024


def sigmoid(value):
    return 0.5 * jnp.tanh(0.5 * value) + 0.5


def vmem():
    return pl.BlockSpec(memory_space=pltpu.VMEM)


def smem():
    return pl.BlockSpec(memory_space=pltpu.SMEM)


def front_kernel(
    own_count, wanted, requests, feat_hbm, adj_hbm, mask, token, weight, bias, gain,
    stack_out, scaled_out, agg_out, slope_out,
    feat, adj, gathered, packed, asked, landed,
    feat_sem, w_send, w_recv, z_send, z_recv,
):
    d = lax.axis_index("dom")
    t = lax.axis_index("tp")
    low = lax.rem(t, 2)
    high = lax.div(t, 2)
    core_peer = high * 2 + (1 - low)
    y_peer = (1 - high) * 2 + low
    a = lax.div(d, wanted)
    j = lax.rem(d, wanted)
    width, quarter = weight.shape
    block = mask.shape[2]

    feat_copy = pltpu.make_async_copy(feat_hbm, feat, feat_sem.at[0])
    adj_copy = pltpu.make_async_copy(adj_hbm, adj, feat_sem.at[1])
    feat_copy.start()
    adj_copy.start()

    barrier = pltpu.get_barrier_semaphore()
    for peer in (core_peer, y_peer):
        pl.semaphore_signal(barrier, inc=1, device_id={"tp": peer}, device_id_type=MESH)

    def pair_of(c):
        return t * wanted + lax.rem(j + c, wanted), a

    for c in range(wanted):
        to_dom, to_tp = pair_of(c)
        back_dom = t * wanted + lax.rem(j - c + wanted, wanted)

        def greet():
            pl.semaphore_signal(barrier, inc=1, device_id=(to_dom, to_tp), device_id_type=MESH)
            pl.semaphore_signal(barrier, inc=1, device_id=(back_dom, to_tp), device_id_type=MESH)

        if c == 0:
            pl.when(a != t)(greet)
        else:
            greet()

    columns = lambda c: pl.ds(pl.multiple_of(c * quarter, quarter), quarter)
    packed[:width, :] = weight[...]
    packed[pl.ds(width, 16), :] = jnp.broadcast_to(bias[...], (16, quarter))
    gathered[:, columns(t)] = packed[...]
    pl.semaphore_wait(barrier, 2 + 2 * wanted - jnp.where(a == t, 2, 0))

    def weight_copy(k, source, column, peer):
        return pltpu.make_async_remote_copy(
            src_ref=source, dst_ref=gathered.at[:, columns(column)],
            send_sem=w_send.at[k], recv_sem=w_recv.at[k],
            device_id={"tp": peer}, device_id_type=MESH,
        )

    across = weight_copy(0, packed, t, y_peer)
    near = weight_copy(1, packed, t, core_peer)
    relay = weight_copy(2, gathered.at[:, columns(y_peer)], y_peer, core_peer)
    across.start()
    near.start()

    rows = lax.broadcasted_iota(jnp.int32, (block, block), 0)
    cols = lax.broadcasted_iota(jnp.int32, (block, block), 1)
    token32 = token[...].astype(jnp.float32)

    def aggregate(node_block, spot):
        hidden = jnp.sum(
            jnp.where(rows == cols, mask[node_block].astype(jnp.float32), 0.0), axis=1, keepdims=True
        )
        masked32 = jnp.where(hidden == 1.0, token32, feat[node_block].astype(jnp.float32))
        mixed = jnp.dot(
            adj[node_block], masked32.astype(jnp.bfloat16), preferred_element_type=jnp.float32
        )
        agg_out[spot] = (masked32 + mixed).astype(jnp.bfloat16)

    feat_copy.wait()
    adj_copy.wait()
    for k in range(wanted):
        aggregate(requests[t * wanted + k], own_count + k)
    across.wait_recv()
    relay.start()
    for k in range(own_count):
        aggregate(t * own_count + k, k)
    near.wait_recv()
    relay.wait_recv()

    matrix = gathered[:width, :]
    shift = gathered[width : width + 1, :].astype(jnp.float32)

    def activate(spot, many):
        agg = agg_out[pl.ds(spot, many)].reshape(many * block, width)
        pre = jnp.dot(agg, matrix, preferred_element_type=jnp.float32) + shift
        sig = sigmoid(pre)
        slope_out[pl.ds(spot, many)] = (sig * (1.0 + pre * (1.0 - sig))).reshape(many, block, width)
        return (pre * sig).astype(jnp.bfloat16).reshape(many, block, width)

    for k in range(wanted):
        asked[k] = activate(own_count + k, 1)[0]

    def z_copy(c):
        return pltpu.make_async_remote_copy(
            src_ref=asked.at[lax.rem(j + c, wanted)], dst_ref=landed.at[j],
            send_sem=z_send.at[c], recv_sem=z_recv.at[c],
            device_id=pair_of(c), device_id_type=MESH,
        )

    pl.when(a != t)(lambda: z_copy(0).start())
    for c in range(1, wanted):
        z_copy(c).start()

    @pl.when(a == t)
    def _():
        landed[j] = asked[j]

    for k in range(0, own_count, 2):
        z = activate(k, 2)
        stack_out[pl.ds(k, 2)] = z
        scaled_out[pl.ds(k, 2)] = (z.astype(jnp.float32) * gain[...][None]).astype(jnp.bfloat16)

    pl.when(a != t)(lambda: z_copy(0).wait())
    for c in range(1, wanted):
        z_copy(c).wait()
    for k in range(wanted):
        stack_out[own_count + k] = landed[k]
    across.wait_send()
    near.wait_send()
    relay.wait_send()


def front(own_count, wanted, requests, feat, adj, mask, token, weight, bias, gain):
    nblocks, block, width = feat.shape
    quarter = weight.shape[1]
    total = own_count + wanted
    dma = pltpu.SemaphoreType.DMA
    anywhere = pl.BlockSpec(memory_space=pltpu.HBM)
    return pl.pallas_call(
        functools.partial(front_kernel, own_count, wanted),
        in_specs=[smem(), anywhere, anywhere] + [vmem()] * 5,
        out_specs=[vmem()] * 4,
        out_shape=(
            jax.ShapeDtypeStruct((total, block, width), jnp.bfloat16),
            jax.ShapeDtypeStruct((own_count, block, width), jnp.bfloat16),
            jax.ShapeDtypeStruct((total, block, width), jnp.bfloat16),
            jax.ShapeDtypeStruct((total, block, width), jnp.float32),
        ),
        scratch_shapes=[
            pltpu.VMEM((nblocks, block, width), jnp.bfloat16),
            pltpu.VMEM((nblocks, block, block), jnp.bfloat16),
            pltpu.VMEM((width + 16, width), jnp.bfloat16),
            pltpu.VMEM((width + 16, quarter), jnp.bfloat16),
            pltpu.VMEM((wanted, block, width), jnp.bfloat16),
            pltpu.VMEM((wanted, block, width), jnp.bfloat16),
            dma((2,)), dma((3,)), dma((3,)), dma((wanted,)), dma((wanted,)),
        ],
        compiler_params=pltpu.CompilerParams(
            collective_id=0, has_side_effects=True, vmem_limit_bytes=VMEM_LIMIT
        ),
    )(requests, feat, adj, mask, token, weight, bias, gain)


def run_pairs(first, second, count, words, stack, scaled, first_acc, second_acc):
    live_count = count[0]
    block = stack.shape[1]
    shifts = lax.broadcasted_iota(jnp.int32, (block // 16, 16, block), 1)

    @pl.loop(0, pl.cdiv(live_count, UNROLL))
    def _(step):
        results = []
        for k in range(UNROLL):
            spot = step * UNROLL + k
            live = spot < live_count
            slot = jnp.where(live, spot, 0)
            ia = first[slot]
            ib = second[slot]
            scaled_a = scaled[ia]
            tile_b = stack[ib]
            logits = lax.dot_general(
                scaled_a, tile_b, (((1,), (1,)), ((), ())), preferred_element_type=jnp.float32
            )
            bits = jnp.bitwise_and(jnp.right_shift(words[slot][:, None, :], shifts), 1)
            label = bits.reshape(block, block).astype(jnp.float32)
            factor = jnp.where(live, INV_NORM, 0.0)
            slope = ((sigmoid(logits) - label) * factor).astype(jnp.bfloat16)
            part_a = jnp.dot(slope, tile_b, preferred_element_type=jnp.float32)
            part_b = lax.dot_general(
                slope, scaled_a, (((0,), (0,)), ((), ())), preferred_element_type=jnp.float32
            )
            results.append((ia, ib, part_a, part_b))
        for ia, ib, part_a, part_b in results:
            first_acc[ia] += part_a
            second_acc[ib] += part_b


def decode_kernel(first, second, count, words, stack, scaled, first_acc, second_out, back_out, second_acc):
    own_count = scaled.shape[0]
    first_acc[...] = jnp.zeros_like(first_acc)
    second_acc[...] = jnp.zeros_like(second_acc)
    run_pairs(first, second, count, words, stack, scaled, first_acc, second_acc)
    second_out[...] = second_acc[:own_count]
    back_out[...] = second_acc[own_count:].astype(jnp.bfloat16)


def decode(first, second, count, words, stack, scaled):
    total, block, width = stack.shape
    own_count = scaled.shape[0]
    return pl.pallas_call(
        decode_kernel,
        in_specs=[smem()] * 3 + [vmem()] * 3,
        out_specs=[vmem()] * 3,
        out_shape=(
            jax.ShapeDtypeStruct((own_count, block, width), jnp.float32),
            jax.ShapeDtypeStruct((own_count, block, width), jnp.float32),
            jax.ShapeDtypeStruct((total - own_count, block, width), jnp.bfloat16),
        ),
        scratch_shapes=[pltpu.VMEM((total, block, width), jnp.float32)],
        compiler_params=pltpu.CompilerParams(vmem_limit_bytes=VMEM_LIMIT),
        cost_estimate=pl.CostEstimate(
            flops=64 * 6 * block * block * width, bytes_accessed=8 << 20, transcendentals=0
        ),
    )(first, second, count, words, stack, scaled)


def reduce_kernel(
    doms, own_count, wanted, first, second, back, stack, agg, slope, gain, weight_out, small_out,
    part, home, dpre, recv_core, sum_core, recv_y, total, recv_dom, recv_small, full,
    core_send, core_recv, y_send, y_recv, dom_send, dom_recv, small_send, small_recv,
    full_send, full_recv, home_send, home_recv,
):
    d = lax.axis_index("dom")
    t = lax.axis_index("tp")
    low = lax.rem(t, 2)
    high = lax.div(t, 2)
    core_peer = high * 2 + (1 - low)
    y_peer = (1 - high) * 2 + low
    width = full.shape[0]
    rows = width // doms

    barrier = pltpu.get_barrier_semaphore()
    for peer in (core_peer, y_peer):
        pl.semaphore_signal(barrier, inc=1, device_id={"tp": peer}, device_id_type=MESH)

    @pl.loop(1, doms)
    def _(o):
        pl.semaphore_signal(
            barrier, inc=1, device_id={"dom": lax.rem(d + o, doms)}, device_id_type=MESH
        )

    a = lax.div(d, wanted)
    j = lax.rem(d, wanted)

    def pair_of(c):
        return t * wanted + lax.rem(j - c + wanted, wanted), a

    for c in range(wanted):
        to_dom, to_tp = pair_of(c)
        from_dom = t * wanted + lax.rem(j + c, wanted)

        def greet():
            pl.semaphore_signal(barrier, inc=1, device_id=(to_dom, to_tp), device_id_type=MESH)
            pl.semaphore_signal(barrier, inc=1, device_id=(from_dom, to_tp), device_id_type=MESH)

        if c == 0:
            pl.when(a != t)(greet)
        else:
            greet()

    pl.semaphore_wait(barrier, doms + 1 + 2 * wanted - jnp.where(a == t, 2, 0))

    def home_copy(c):
        return pltpu.make_async_remote_copy(
            src_ref=back.at[lax.rem(j - c + wanted, wanted)], dst_ref=home.at[j],
            send_sem=home_send.at[c], recv_sem=home_recv.at[c],
            device_id=pair_of(c), device_id_type=MESH,
        )

    pl.when(a != t)(lambda: home_copy(0).start())
    for c in range(1, wanted):
        home_copy(c).start()

    @pl.when(a == t)
    def _():
        home[j] = back[j]

    block = stack.shape[1]
    bias_sum = jnp.zeros((1, width), jnp.float32)
    gain_sum = jnp.zeros((1, width), jnp.float32)
    for k in range(own_count):
        value = first[k]
        gain_sum += jnp.sum(stack[k].astype(jnp.float32) * value, axis=0, keepdims=True)
        value = (gain[...] * value + second[k]) * slope[k]
        bias_sum += jnp.sum(value, axis=0, keepdims=True)
        dpre[pl.ds(k * block, block), :] = value.astype(jnp.bfloat16)

    lanes, _, quarter = part.shape

    def product(start, many, c):
        left = agg[pl.ds(start, many)].reshape(many * block, width)
        right = dpre[pl.ds(start * block, many * block), pl.ds(c * quarter, 2 * quarter)]
        return lax.dot_general(
            left, right, (((0,), (0,)), ((), ())), preferred_element_type=jnp.float32
        )

    for c in range(0, lanes, 2):
        both = product(0, own_count, c)
        for k in range(2):
            part[c + k, :width, :] = both[:, k * quarter : (k + 1) * quarter]

    pl.when(a != t)(lambda: home_copy(0).wait())
    for c in range(1, wanted):
        home_copy(c).wait()
    for k in range(wanted):
        value = home[k].astype(jnp.float32) * slope[own_count + k]
        bias_sum += jnp.sum(value, axis=0, keepdims=True)
        dpre[pl.ds((own_count + k) * block, block), :] = value.astype(jnp.bfloat16)
    for c in range(0, lanes, 2):
        both = product(own_count, wanted, c)
        for k in range(2):
            part[c + k, :width, :] += both[:, k * quarter : (k + 1) * quarter]
    row = lax.broadcasted_iota(jnp.int32, (8, width), 0)
    extra = jnp.where(row == 0, bias_sum, jnp.where(row == 1, gain_sum, 0.0))
    for c in range(lanes):
        part[c, pl.ds(width, 8), :] = extra[:, c * quarter : (c + 1) * quarter]

    def core_copy(h):
        return pltpu.make_async_remote_copy(
            src_ref=part.at[2 * h + 1 - low], dst_ref=recv_core.at[h],
            send_sem=core_send.at[h], recv_sem=core_recv.at[h],
            device_id={"tp": core_peer}, device_id_type=MESH,
        )

    def y_copy():
        return pltpu.make_async_remote_copy(
            src_ref=sum_core, dst_ref=recv_y, send_sem=y_send, recv_sem=y_recv,
            device_id={"tp": y_peer}, device_id_type=MESH,
        )

    far = core_copy(1 - high)
    near = core_copy(high)
    far.start()
    near.start()
    far.wait_recv()
    sum_core[...] = part[2 * (1 - high) + low] + recv_core[1 - high]
    across = y_copy()
    across.start()
    near.wait_recv()
    total[...] = part[2 * high + low] + recv_core[high]
    across.wait()
    total[...] += recv_y[...]

    def dom_copy(o):
        peer = lax.rem(d + o, doms)
        return pltpu.make_async_remote_copy(
            src_ref=total.at[pl.ds(pl.multiple_of(peer * rows, 8), rows)], dst_ref=recv_dom.at[o],
            send_sem=dom_send.at[o], recv_sem=dom_recv.at[o],
            device_id={"dom": peer}, device_id_type=MESH,
        )

    def small_copy(o):
        peer = lax.rem(d + o, doms)
        return pltpu.make_async_remote_copy(
            src_ref=total.at[pl.ds(width, 8)], dst_ref=recv_small.at[d],
            send_sem=small_send.at[o], recv_sem=small_recv.at[o],
            device_id={"dom": peer}, device_id_type=MESH,
        )

    @pl.loop(1, doms)
    def _(o):
        dom_copy(o).start()

    @pl.loop(1, doms)
    def _(o):
        small_copy(o).start()

    mine = pl.ds(pl.multiple_of(d * rows, 8), rows)
    full[mine, :] = total[mine, :]
    recv_small[d] = total[pl.ds(width, 8), :]

    @pl.loop(1, doms)
    def _(o):
        dom_copy(o).wait()
        full[mine, :] += recv_dom[o]

    def full_copy(o):
        return pltpu.make_async_remote_copy(
            src_ref=full.at[mine], dst_ref=full.at[mine],
            send_sem=full_send.at[o], recv_sem=full_recv.at[o],
            device_id={"dom": lax.rem(d + o, doms)}, device_id_type=MESH,
        )

    @pl.loop(1, doms)
    def _(o):
        full_copy(o).start()

    @pl.loop(1, doms)
    def _(o):
        small_copy(o).wait()

    small = recv_small[0]
    for k in range(1, doms):
        small += recv_small[k]
    small_out[...] = small

    @pl.loop(1, doms)
    def _(o):
        full_copy(o).wait()

    far.wait_send()
    near.wait_send()
    weight_out[...] = full[...]


def reduce_all(doms, lanes, first, second, back, stack, agg, slope, gain):
    own_count, block, width = first.shape
    wanted = back.shape[0]
    quarter = width // lanes
    tall = width + 8
    rows = width // doms
    dma = pltpu.SemaphoreType.DMA
    return pl.pallas_call(
        functools.partial(reduce_kernel, doms, own_count, wanted),
        in_specs=[vmem()] * 7,
        out_specs=[vmem()] * 2,
        out_shape=(
            jax.ShapeDtypeStruct((width, quarter), jnp.float32),
            jax.ShapeDtypeStruct((8, quarter), jnp.float32),
        ),
        scratch_shapes=[
            pltpu.VMEM((lanes, tall, quarter), jnp.float32),
            pltpu.VMEM((wanted, block, width), jnp.bfloat16),
            pltpu.VMEM(((own_count + wanted) * block, width), jnp.bfloat16),
            pltpu.VMEM((2, tall, quarter), jnp.float32),
            pltpu.VMEM((tall, quarter), jnp.float32),
            pltpu.VMEM((tall, quarter), jnp.float32),
            pltpu.VMEM((tall, quarter), jnp.float32),
            pltpu.VMEM((doms, rows, quarter), jnp.float32),
            pltpu.VMEM((doms, 8, quarter), jnp.float32),
            pltpu.VMEM((width, quarter), jnp.float32),
            dma((2,)), dma((2,)), dma, dma,
            dma((doms,)), dma((doms,)), dma((doms,)), dma((doms,)), dma((doms,)), dma((doms,)),
            dma((wanted,)), dma((wanted,)),
        ],
        compiler_params=pltpu.CompilerParams(
            collective_id=1, has_side_effects=True, vmem_limit_bytes=VMEM_LIMIT
        ),
    )(first, second, back, stack, agg, slope, gain)


def body(
    features, adjacency, node_mask, mask_token, enc_weight, enc_bias, gain, requests,
    pair_first, pair_second, label_words, pair_count,
):
    nodes, width = features.shape
    block = adjacency.shape[1]
    nblocks = nodes // block
    doms = lax.axis_size("dom")
    lanes = lax.axis_size("tp")
    own_count = nblocks // lanes
    wanted = doms // lanes
    gain_row = gain.reshape(1, width)
    stack, scaled, agg, slope = front(
        own_count, wanted, requests.reshape(doms),
        features.reshape(nblocks, block, width),
        adjacency.reshape(nblocks, block, block),
        node_mask.reshape(nblocks, 1, block),
        mask_token.reshape(1, width), enc_weight, enc_bias.reshape(1, -1), gain_row,
    )
    first, second, back = decode(
        pair_first[0, 0], pair_second[0, 0], pair_count.reshape(1), label_words[0, 0], stack, scaled
    )
    weight_grad, small = reduce_all(doms, lanes, first, second, back, stack, agg, slope, gain_row)
    return weight_grad, small[0], small[1]


def solution(mesh):
    placed = (
        P("dom", None),
        P("dom", None),
        P("dom"),
        P(),
        P(None, "tp"),
        P("tp"),
        P(),
        P(None, "dom"),
        P("dom", "tp", None),
        P("dom", "tp", None),
        P("dom", "tp", None, None, None),
        P("dom", "tp"),
    )
    return jax.shard_map(
        body,
        mesh=mesh,
        in_specs=placed,
        out_specs=(P(None, "tp"), P("tp"), P("tp")),
        check_vma=False,
    )
```

time: 391 us -> 92.4 us (0.24)
  waiting for transfers between devices: 96 us -> 0 us
  other arithmetic: 95.6 us -> 0 us
  Pallas kernels: 0 us -> 81.7 us
  local copies, waits for them, and re-layouts: 73.2 us -> 8.94 us
  matrix products: 45.7 us -> 0 us
  blocking collectives: 36.4 us -> 0 us
  starting transfers between devices: 20.5 us -> 0 us
  between operations: 14.3 us -> 1.35 us
  loops' own time: 5.86 us -> 0 us
    pallas_call x0 -> x3, Pallas kernels: none -> 81.7 us  [the longest x1 54.2 us: reduce_all(): pl.pallas_call(functools.partial(reduce_kernel, doms, own_count, wanted),...]
    scatter-add x16 -> x0, other arithmetic: 67.2 us -> none  [the longest x8 33.9 us: step(): second_acc.at[index_b].add(part_b)]
    psum x1 -> x0, waiting for transfers between devices: 48 us -> none  [body(): lax.psum((weight_part, bias_part, gain_sum), 'dom')]
    dot_general x28 -> x0, matrix products: 45.7 us -> none  [the longest x8 13.7 us: step(): jnp.einsum('pij,pif->pjf', slope, scaled, preferred_element_type=jnp.floa...]
    all_to_all x5 -> x0, waiting for transfers between devices: 38 us -> none  [the longest x1 24.9 us: body(): lax.all_to_all(local_grad, 'tp', split_axis=2, concat_axis=0, tiled=True)]
    gather x17 -> x0, local copies, waits for them, and re-layouts: 35.7 us -> none  [the longest x8 18.4 us: step(): tile_a = stack[index_a]]
    all_to_all x5 -> x0, starting transfers between devices: 20.4 us -> none  [the longest x1 5.71 us: body(): lax.all_to_all(lax.all_to_all(second_acc[own_count:].astype(jnp.bfloat16)...]
    psum x1 -> x0, blocking collectives: 20.4 us -> none  [body(): lax.psum((weight_part, bias_part, gain_sum), 'dom')]
  transfers between devices with their start and end apart: 7 -> 0, of which waited for: 6 -> 0; matrix products, arithmetic and copies ran while one was open for 5% -> 0% of each run, Pallas kernels for 0% -> 0%
where the time goes in v1:
time: 92.4 us; the launch traced here: 91.9 us
  Pallas kernels  81.7 us (88%)
  local copies, waits for them, and re-layouts  8.94 us (10%)
  between operations  1.35 us (1%)
    pallas_call x1, Pallas kernels, reduce_all(): pl.pallas_call(functools.partial(reduce_kernel, doms, own_count, wanted),...  54.2 us
    pallas_call x1, Pallas kernels, front(): pl.pallas_call(functools.partial(front_kernel, own_count, wanted), in_spe...  16.5 us
    pallas_call x1, Pallas kernels, decode(): pl.pallas_call(decode_kernel, in_specs=[smem()] * 3 + [vmem()] * 3, out_s...  10.9 us
    unnamed x23, local copies, waits for them, and re-layouts  7.74 us

profile of v1, /device:TPU:0, one launch (start us, length us, event | category | flops | bytes accessed | tf_op | source)
XLA Modules:
  0.0 91.9 jit_solution(12579584523324923426)
XLA Ops:
  1.3 0.7 reshape.35.token
  2.0 0.0 copy-start
  2.0 2.2 %copy-done = bf16[4096,512]{1,0:T(8,128)(2,1)S(1)} copy-done((bf16[4096,512]{1,0:T(8,128)(2,1)S(1)}, bf16[4096,512]{1,0:T(8,128)(2,1)}, u32[]{:S(2)}) %copy-start) | copy-done | bytes 4194328
  4.1 0.0 copy-start.1
  4.2 1.2 %copy-done.1 = bf16[4096,128]{1,0:T(8,128)(2,1)S(1)} copy-done((bf16[4096,128]{1,0:T(8,128)(2,1)S(1)}, bf16[4096,128]{1,0:T(8,128)(2,1)}, u32[]{:S(2)}) %copy-start.1) | copy-done | bytes 1048600
  5.4 0.0 copy-start.2
  5.4 0.9 copy-done.2
  6.3 0.0 copy-start.3
  6.3 0.7 copy-done.3
  7.0 0.0 copy-start.4
  7.0 0.7 copy-done.4
  7.7 0.0 copy-start.6
  7.7 0.7 copy-done.6
  8.3 0.0 copy-start.7
  8.3 0.7 copy-done.7
  9.0 0.0 copy-start.8
  9.0 0.0 copy-start.9
  9.0 0.0 copy-start.10
  9.0 16.5 %shard_map.139 = (bf16[10,128,512]{2,1,0:T(8,128)(2,1)S(1)}, bf16[8,128,512]{2,1,0:T(8,128)(2,1)S(1)}, bf16[10,128,512]{2,1,0:T(8,128)(2,1)S(1)}, f32[10,128,512]{2,1,0:T(8,128)S(1)}) custom-call(s32[8]{0:T(128)S(1)} %bitcast.20, bf16[32,128,512]{2,1,0:T(8,128)(2,1)S(1)} %bitcast.15, bf16[32,128,128]{2,1,0:T(8,128)(2,1)S(1)} %bitcast.16, ...), custom_call_target="tpu_custom_call" | custom-call | tf_op jit(solution)/shard_map/pallas_call | solution.py:163
  25.5 0.0 copy-done.8
  25.5 0.0 copy-done.9
  25.6 0.0 copy-done.10
  25.6 0.0 copy-start.5
  25.6 10.9 %shard_map.140 = (f32[8,128,512]{2,1,0:T(8,128)S(1)}, f32[8,128,512]{2,1,0:T(8,128)S(1)}, bf16[2,128,512]{2,1,0:T(8,128)(2,1)S(1)}) custom-call(s32[64]{0:T(128)S(1)} %bitcast.23, s32[64]{0:T(128)S(1)} %bitcast.24, s32[1]{0:T(128)} %bitcast.14.count, s32[64,8,128]{2,1,0:T(8,128)S(1)} %bitcast.22, bf16[10,128,512]{2,1,0:T(8,128)(2,1)S(1)} %get-tuple-element.12.stack, ...), custom_call_target="tpu_custom_call" | custom-call | flops 3221225472 | bytes 8388608 | tf_op jit(solution)/shard_map/pallas_call | solution.py:233
  36.5 0.0 copy-done.5
  36.5 54.2 %shard_map.141 = (f32[512,128]{1,0:T(8,128)S(1)}, f32[8,128]{1,0:T(8,128)S(1)}) custom-call(f32[8,128,512]{2,1,0:T(8,128)S(1)} %get-tuple-element.14.first, f32[8,128,512]{2,1,0:T(8,128)S(1)} %get-tuple-element.15.second, bf16[2,128,512]{2,1,0:T(8,128)(2,1)S(1)} %get-tuple-element.16.back, bf16[10,128,512]{2,1,0:T(8,128)(2,1)S(1)} %get-tuple-element.12.stack, ...), custom_call_target="tpu_custom_call" | custom-call | tf_op jit(solution)/shard_map/pallas_call | solution.py:446
  90.7 0.5 slice_bitcast_fusion
  91.2 0.7 copy.17
Async XLA Ops:
  2.0 2.2 %copy-start = (bf16[4096,512]{1,0:T(8,128)(2,1)S(1)}, bf16[4096,512]{1,0:T(8,128)(2,1)}, u32[]{:S(2)}) copy-start(bf16[4096,512]{1,0:T(8,128)(2,1)} %param.12) | copy-start | bytes 12582916
  4.1 1.2 %copy-start.1 = (bf16[4096,128]{1,0:T(8,128)(2,1)S(1)}, bf16[4096,128]{1,0:T(8,128)(2,1)}, u32[]{:S(2)}) copy-start(bf16[4096,128]{1,0:T(8,128)(2,1)} %param.13) | copy-start | bytes 3145732
  5.4 0.9 copy-start.2
  6.3 0.7 copy-start.3
  7.0 0.7 copy-start.4
  7.7 0.7 copy-start.6
  8.3 0.7 copy-start.7
  9.0 16.5 %copy-start.8 = (s32[1,1,64,8,128]{4,3,2,1,0:T(8,128)S(1)}, s32[1,1,64,8,128]{4,3,2,1,0:T(8,128)}, u32[]{:S(2)}) copy-start(s32[1,1,64,8,128]{4,3,2,1,0:T(8,128)} %param.22) | copy-start | bytes 786436
  9.0 16.6 %copy-start.9 = (s32[1,1,64]{2,1,0:T(1,128)S(1)}, s32[1,1,64]{2,1,0:T(1,128)}, u32[]{:S(2)}) copy-start(s32[1,1,64]{2,1,0:T(1,128)} %param.20) | copy-start | bytes 772
  9.0 16.6 %copy-start.10 = (s32[1,1,64]{2,1,0:T(1,128)S(1)}, s32[1,1,64]{2,1,0:T(1,128)}, u32[]{:S(2)}) copy-start(s32[1,1,64]{2,1,0:T(1,128)} %param.21) | copy-start | bytes 772
  25.6 10.9 %copy-start.5 = (f32[512]{0:T(512)S(1)}, f32[512]{0:T(512)}, u32[]{:S(2)}) copy-start(f32[512]{0:T(512)} %param.18) | copy-start | bytes 6148

commit v2 on v1

--- a/solution.py
+++ b/solution.py
@@ -11,12 +11,17 @@
 INV_NORM = 1.0 / 256.0
 MESH = pl.DeviceIdType.MESH
 VMEM_LIMIT = 32 * 1024 * 1024
+FRONT_LIMIT = 60 * 1024 * 1024
 
 
 def sigmoid(value):
     return 0.5 * jnp.tanh(0.5 * value) + 0.5
 
 
+def served(lane):
+    return lax.rem(lane, 2) * 2 + lax.div(lane, 2)
+
+
 def vmem():
     return pl.BlockSpec(memory_space=pltpu.VMEM)
 
@@ -26,9 +31,9 @@
 
 
 def front_kernel(
-    own_count, wanted, requests, feat_hbm, adj_hbm, mask, token, weight, bias, gain,
+    own_count, wanted, requests, feat_hbm, adj_hbm, mask_hbm, token_hbm, weight_hbm, bias_hbm, gain_hbm,
     stack_out, scaled_out, agg_out, slope_out,
-    feat, adj, gathered, packed, asked, landed,
+    feat, adj, mask, token, bias, gain, gathered, packed, asked, landed,
     feat_sem, w_send, w_recv, z_send, z_recv,
 ):
     d = lax.axis_index("dom")
@@ -39,39 +44,53 @@
     y_peer = (1 - high) * 2 + low
     a = lax.div(d, wanted)
     j = lax.rem(d, wanted)
-    width, quarter = weight.shape
+    width, quarter = weight_hbm.shape
     block = mask.shape[2]
 
-    feat_copy = pltpu.make_async_copy(feat_hbm, feat, feat_sem.at[0])
-    adj_copy = pltpu.make_async_copy(adj_hbm, adj, feat_sem.at[1])
-    feat_copy.start()
-    adj_copy.start()
+    fetches = [
+        pltpu.make_async_copy(source, target, feat_sem.at[k])
+        for k, (source, target) in enumerate(
+            (
+                (weight_hbm, packed.at[pl.ds(0, width)]),
+                (bias_hbm, bias),
+                (token_hbm, token),
+                (mask_hbm, mask),
+                (adj_hbm, adj),
+                (feat_hbm, feat),
+                (gain_hbm, gain),
+            )
+        )
+    ]
+    for fetch in fetches:
+        fetch.start()
 
     barrier = pltpu.get_barrier_semaphore()
     for peer in (core_peer, y_peer):
         pl.semaphore_signal(barrier, inc=1, device_id={"tp": peer}, device_id_type=MESH)
 
     def pair_of(c):
-        return t * wanted + lax.rem(j + c, wanted), a
-
+        return served(t) * wanted + lax.rem(j + c, wanted), a
+
+    alone = jnp.logical_and(a == t, served(t) == t)
     for c in range(wanted):
-        to_dom, to_tp = pair_of(c)
-        back_dom = t * wanted + lax.rem(j - c + wanted, wanted)
+        target = pair_of(c)
+        source = t * wanted + lax.rem(j - c + wanted, wanted), served(a)
 
         def greet():
-            pl.semaphore_signal(barrier, inc=1, device_id=(to_dom, to_tp), device_id_type=MESH)
-            pl.semaphore_signal(barrier, inc=1, device_id=(back_dom, to_tp), device_id_type=MESH)
+            pl.semaphore_signal(barrier, inc=1, device_id=target, device_id_type=MESH)
+            pl.semaphore_signal(barrier, inc=1, device_id=source, device_id_type=MESH)
 
         if c == 0:
-            pl.when(a != t)(greet)
+            pl.when(jnp.logical_not(alone))(greet)
         else:
             greet()
 
     columns = lambda c: pl.ds(pl.multiple_of(c * quarter, quarter), quarter)
-    packed[:width, :] = weight[...]
+    fetches[0].wait()
+    fetches[1].wait()
     packed[pl.ds(width, 16), :] = jnp.broadcast_to(bias[...], (16, quarter))
     gathered[:, columns(t)] = packed[...]
-    pl.semaphore_wait(barrier, 2 + 2 * wanted - jnp.where(a == t, 2, 0))
+    pl.semaphore_wait(barrier, 2 + 2 * wanted - jnp.where(alone, 2, 0))
 
     def weight_copy(k, source, column, peer):
         return pltpu.make_async_remote_copy(
@@ -88,6 +107,8 @@
 
     rows = lax.broadcasted_iota(jnp.int32, (block, block), 0)
     cols = lax.broadcasted_iota(jnp.int32, (block, block), 1)
+    for fetch in fetches[2:]:
+        fetch.wait()
     token32 = token[...].astype(jnp.float32)
 
     def aggregate(node_block, spot):
@@ -100,10 +121,8 @@
         )
         agg_out[spot] = (masked32 + mixed).astype(jnp.bfloat16)
 
-    feat_copy.wait()
-    adj_copy.wait()
     for k in range(wanted):
-        aggregate(requests[t * wanted + k], own_count + k)
+        aggregate(requests[served(t) * wanted + k], own_count + k)
     across.wait_recv()
     relay.start()
     for k in range(own_count):
@@ -131,11 +150,11 @@
             device_id=pair_of(c), device_id_type=MESH,
         )
 
-    pl.when(a != t)(lambda: z_copy(0).start())
+    pl.when(jnp.logical_not(alone))(lambda: z_copy(0).start())
     for c in range(1, wanted):
         z_copy(c).start()
 
-    @pl.when(a == t)
+    @pl.when(alone)
     def _():
         landed[j] = asked[j]
 
@@ -144,7 +163,7 @@
         stack_out[pl.ds(k, 2)] = z
         scaled_out[pl.ds(k, 2)] = (z.astype(jnp.float32) * gain[...][None]).astype(jnp.bfloat16)
 
-    pl.when(a != t)(lambda: z_copy(0).wait())
+    pl.when(jnp.logical_not(alone))(lambda: z_copy(0).wait())
     for c in range(1, wanted):
         z_copy(c).wait()
     for k in range(wanted):
@@ -162,7 +181,7 @@
     anywhere = pl.BlockSpec(memory_space=pltpu.HBM)
     return pl.pallas_call(
         functools.partial(front_kernel, own_count, wanted),
-        in_specs=[smem(), anywhere, anywhere] + [vmem()] * 5,
+        in_specs=[smem()] + [anywhere] * 7,
         out_specs=[vmem()] * 4,
         out_shape=(
             jax.ShapeDtypeStruct((total, block, width), jnp.bfloat16),
@@ -173,14 +192,18 @@
         scratch_shapes=[
             pltpu.VMEM((nblocks, block, width), jnp.bfloat16),
             pltpu.VMEM((nblocks, block, block), jnp.bfloat16),
+            pltpu.VMEM((nblocks, 1, block), jnp.int32),
+            pltpu.VMEM((1, width), jnp.bfloat16),
+            pltpu.VMEM((1, quarter), jnp.bfloat16),
+            pltpu.VMEM((1, width), jnp.float32),
             pltpu.VMEM((width + 16, width), jnp.bfloat16),
             pltpu.VMEM((width + 16, quarter), jnp.bfloat16),
             pltpu.VMEM((wanted, block, width), jnp.bfloat16),
             pltpu.VMEM((wanted, block, width), jnp.bfloat16),
-            dma((2,)), dma((3,)), dma((3,)), dma((wanted,)), dma((wanted,)),
+            dma((7,)), dma((3,)), dma((3,)), dma((wanted,)), dma((wanted,)),
         ],
         compiler_params=pltpu.CompilerParams(
-            collective_id=0, has_side_effects=True, vmem_limit_bytes=VMEM_LIMIT
+            collective_id=0, has_side_effects=True, vmem_limit_bytes=FRONT_LIMIT
         ),
     )(requests, feat, adj, mask, token, weight, bias, gain)
 
@@ -248,7 +271,7 @@
 
 
 def reduce_kernel(
-    doms, own_count, wanted, first, second, back, stack, agg, slope, gain, weight_out, small_out,
+    doms, own_count, wanted, first, second, back, stack, agg, slope, gain, weight_out, bias_out, gain_out,
     part, home, dpre, recv_core, sum_core, recv_y, total, recv_dom, recv_small, full,
     core_send, core_recv, y_send, y_recv, dom_send, dom_recv, small_send, small_recv,
     full_send, full_recv, home_send, home_recv,
@@ -276,22 +299,23 @@
     j = lax.rem(d, wanted)
 
     def pair_of(c):
-        return t * wanted + lax.rem(j - c + wanted, wanted), a
-
+        return t * wanted + lax.rem(j - c + wanted, wanted), served(a)
+
+    alone = jnp.logical_and(a == t, served(t) == t)
     for c in range(wanted):
-        to_dom, to_tp = pair_of(c)
-        from_dom = t * wanted + lax.rem(j + c, wanted)
+        target = pair_of(c)
+        source = served(t) * wanted + lax.rem(j + c, wanted), a
 
         def greet():
-            pl.semaphore_signal(barrier, inc=1, device_id=(to_dom, to_tp), device_id_type=MESH)
-            pl.semaphore_signal(barrier, inc=1, device_id=(from_dom, to_tp), device_id_type=MESH)
+            pl.semaphore_signal(barrier, inc=1, device_id=target, device_id_type=MESH)
+            pl.semaphore_signal(barrier, inc=1, device_id=source, device_id_type=MESH)
 
         if c == 0:
-            pl.when(a != t)(greet)
+            pl.when(jnp.logical_not(alone))(greet)
         else:
             greet()
 
-    pl.semaphore_wait(barrier, doms + 1 + 2 * wanted - jnp.where(a == t, 2, 0))
+    pl.semaphore_wait(barrier, doms + 1 + 2 * wanted - jnp.where(alone, 2, 0))
 
     def home_copy(c):
         return pltpu.make_async_remote_copy(
@@ -300,11 +324,11 @@
             device_id=pair_of(c), device_id_type=MESH,
         )
 
-    pl.when(a != t)(lambda: home_copy(0).start())
+    pl.when(jnp.logical_not(alone))(lambda: home_copy(0).start())
     for c in range(1, wanted):
         home_copy(c).start()
 
-    @pl.when(a == t)
+    @pl.when(alone)
     def _():
         home[j] = back[j]
 
@@ -332,7 +356,7 @@
         for k in range(2):
             part[c + k, :width, :] = both[:, k * quarter : (k + 1) * quarter]
 
-    pl.when(a != t)(lambda: home_copy(0).wait())
+    pl.when(jnp.logical_not(alone))(lambda: home_copy(0).wait())
     for c in range(1, wanted):
         home_copy(c).wait()
     for k in range(wanted):
@@ -425,7 +449,8 @@
     small = recv_small[0]
     for k in range(1, doms):
         small += recv_small[k]
-    small_out[...] = small
+    bias_out[...] = small[0:1]
+    gain_out[...] = small[1:2]
 
     @pl.loop(1, doms)
     def _(o):
@@ -446,10 +471,11 @@
     return pl.pallas_call(
         functools.partial(reduce_kernel, doms, own_count, wanted),
         in_specs=[vmem()] * 7,
-        out_specs=[vmem()] * 2,
+        out_specs=[vmem()] * 3,
         out_shape=(
             jax.ShapeDtypeStruct((width, quarter), jnp.float32),
-            jax.ShapeDtypeStruct((8, quarter), jnp.float32),
+            jax.ShapeDtypeStruct((1, quarter), jnp.float32),
+            jax.ShapeDtypeStruct((1, quarter), jnp.float32),
         ),
         scratch_shapes=[
             pltpu.VMEM((lanes, tall, quarter), jnp.float32),
@@ -494,8 +520,8 @@
     first, second, back = decode(
         pair_first[0, 0], pair_second[0, 0], pair_count.reshape(1), label_words[0, 0], stack, scaled
     )
-    weight_grad, small = reduce_all(doms, lanes, first, second, back, stack, agg, slope, gain_row)
-    return weight_grad, small[0], small[1]
+    weight_grad, bias_grad, gain_grad = reduce_all(doms, lanes, first, second, back, stack, agg, slope, gain_row)
+    return weight_grad, bias_grad.reshape(-1), gain_grad.reshape(-1)
 
 
 def solution(mesh):

time: 92.4 us -> 89.2 us (0.965)
  local copies, waits for them, and re-layouts: 8.94 us -> 5.55 us
    pallas_call x1, Pallas kernels: 54.2 us -> 43 us  [reduce_all(): pl.pallas_call(functools.partial(reduce_kernel, doms, own_count, wanted),...]
    pallas_call x1, Pallas kernels: 10.9 us -> 19.5 us  [decode(): pl.pallas_call(decode_kernel, in_specs=[smem()] * 3 + [vmem()] * 3, out_s...]
    unnamed x23 -> x21, local copies, waits for them, and re-layouts: 7.74 us -> 4.29 us
    pallas_call x1, Pallas kernels: 16.5 us -> 19.1 us  [front(): pl.pallas_call(functools.partial(front_kernel, own_count, wanted), in_spe...]
where the time goes in v2:
time: 89.2 us; the launch traced here: 88.5 us
  Pallas kernels  81.6 us (91%)
  local copies, waits for them, and re-layouts  5.55 us (6%)
  between operations  1.37 us (2%)
    pallas_call x1, Pallas kernels, reduce_all(): pl.pallas_call(functools.partial(reduce_kernel, doms, own_count, wanted),...  43 us
    pallas_call x1, Pallas kernels, decode(): pl.pallas_call(decode_kernel, in_specs=[smem()] * 3 + [vmem()] * 3, out_s...  19.5 us
    pallas_call x1, Pallas kernels, front(): pl.pallas_call(functools.partial(front_kernel, own_count, wanted), in_spe...  19.1 us
    unnamed x21, local copies, waits for them, and re-layouts  4.29 us

profile of v2, /device:TPU:0, one launch (start us, length us, event | category | flops | bytes accessed | tf_op | source)
XLA Modules:
  0.0 88.5 jit_solution(10101632711547305762)
XLA Ops:
  1.3 1.3 %reshape.41.token_hbm = bf16[1,512]{1,0:T(2,128)(2,1)} reshape(bf16[512]{0:T(512)(128)(2,1)} %param.15) | data formatting | bytes 2048 | tf_op jit(solution)/shard_map/reshape | solution.py:518
  2.5 0.0 copy-start.6
  2.5 0.0 copy-start.7
  2.5 0.0 copy-start.8
  2.5 19.1 %shard_map.139 = (bf16[10,128,512]{2,1,0:T(8,128)(2,1)}, bf16[8,128,512]{2,1,0:T(8,128)(2,1)}, bf16[10,128,512]{2,1,0:T(8,128)(2,1)}, f32[10,128,512]{2,1,0:T(8,128)}) custom-call(s32[8]{0:T(128)} %bitcast.23, bf16[32,128,512]{2,1,0:T(8,128)(2,1)} %bitcast.20, bf16[32,128,128]{2,1,0:T(8,128)(2,1)} %bitcast.21, s32[32,1,128]{2,1,0:T(1,128)} %bitcast.22, ...), custom_call_target="tpu_custom_call" | custom-call | tf_op jit(solution)/shard_map/pallas_call | solution.py:182
  21.6 0.0 copy-done.6
  21.6 0.0 copy-done.7
  21.6 0.0 copy-done.8
  21.6 0.0 copy-start.1
  21.7 1.3 %copy-done.1 = bf16[10,128,512]{2,1,0:T(8,128)(2,1)S(1)} copy-done((bf16[10,128,512]{2,1,0:T(8,128)(2,1)S(1)}, bf16[10,128,512]{2,1,0:T(8,128)(2,1)}, u32[]{:S(2)}) %copy-start.1) | copy-done | bytes 1310744
  23.0 0.0 copy-start.5
  23.0 1.2 %copy-done.5 = bf16[8,128,512]{2,1,0:T(8,128)(2,1)S(1)} copy-done((bf16[8,128,512]{2,1,0:T(8,128)(2,1)S(1)}, bf16[8,128,512]{2,1,0:T(8,128)(2,1)}, u32[]{:S(2)}) %copy-start.5) | copy-done | bytes 1048600
  24.2 0.0 copy-start
  24.2 0.0 copy-start.2
  24.2 0.0 copy-start.3
  24.2 0.0 copy-start.4
  24.2 19.5 %shard_map.140 = (f32[8,128,512]{2,1,0:T(8,128)S(1)}, f32[8,128,512]{2,1,0:T(8,128)S(1)}, bf16[2,128,512]{2,1,0:T(8,128)(2,1)S(1)}) custom-call(s32[64]{0:T(128)S(1)} %bitcast.16, s32[64]{0:T(128)S(1)} %bitcast.17, s32[1]{0:T(128)} %bitcast.12.count, s32[64,8,128]{2,1,0:T(8,128)S(1)} %bitcast.15, bf16[10,128,512]{2,1,0:T(8,128)(2,1)S(1)} %copy-done.1, ...), custom_call_target="tpu_custom_call" | custom-call | flops 3221225472 | bytes 8388608 | tf_op jit(solution)/shard_map/pallas_call | solution.py:256
  43.7 0.0 copy-done
  43.8 0.0 copy-done.2
  43.8 0.0 copy-done.3
  43.8 0.0 copy-done.4
  43.8 43.0 %shard_map.141 = (f32[512,128]{1,0:T(8,128)S(1)}, f32[1,128]{1,0:T(1,128)S(1)}, f32[1,128]{1,0:T(1,128)S(1)}) custom-call(f32[8,128,512]{2,1,0:T(8,128)S(1)} %get-tuple-element.15.first, f32[8,128,512]{2,1,0:T(8,128)S(1)} %get-tuple-element.16.second, bf16[2,128,512]{2,1,0:T(8,128)(2,1)S(1)} %get-tuple-element.17.back, bf16[10,128,512]{2,1,0:T(8,128)(2,1)S(1)} %copy-done.2, ...), custom_call_target="tpu_custom_call" | custom-call | tf_op jit(solution)/shard_map/pallas_call | solution.py:471
  86.8 0.7 copy.19
  87.5 0.5 copy.20
  88.0 0.5 copy.21
Async XLA Ops:
  2.5 19.1 %copy-start.6 = (s32[1,1,64,8,128]{4,3,2,1,0:T(8,128)S(1)}, s32[1,1,64,8,128]{4,3,2,1,0:T(8,128)}, u32[]{:S(2)}) copy-start(s32[1,1,64,8,128]{4,3,2,1,0:T(8,128)} %param.22) | copy-start | bytes 786436
  2.5 19.1 %copy-start.7 = (s32[1,1,64]{2,1,0:T(1,128)S(1)}, s32[1,1,64]{2,1,0:T(1,128)}, u32[]{:S(2)}) copy-start(s32[1,1,64]{2,1,0:T(1,128)} %param.20) | copy-start | bytes 772
  2.5 19.1 %copy-start.8 = (s32[1,1,64]{2,1,0:T(1,128)S(1)}, s32[1,1,64]{2,1,0:T(1,128)}, u32[]{:S(2)}) copy-start(s32[1,1,64]{2,1,0:T(1,128)} %param.21) | copy-start | bytes 772
  21.6 1.3 %copy-start.1 = (bf16[10,128,512]{2,1,0:T(8,128)(2,1)S(1)}, bf16[10,128,512]{2,1,0:T(8,128)(2,1)}, u32[]{:S(2)}) copy-start(bf16[10,128,512]{2,1,0:T(8,128)(2,1)} %get-tuple-element.13.stack) | copy-start | bytes 3932164
  23.0 1.2 %copy-start.5 = (bf16[8,128,512]{2,1,0:T(8,128)(2,1)S(1)}, bf16[8,128,512]{2,1,0:T(8,128)(2,1)}, u32[]{:S(2)}) copy-start(bf16[8,128,512]{2,1,0:T(8,128)(2,1)} %get-tuple-element.14.scaled) | copy-start | bytes 3145732
  24.2 19.6 %copy-start = (f32[10,128,512]{2,1,0:T(8,128)S(1)}, f32[10,128,512]{2,1,0:T(8,128)}, u32[]{:S(2)}) copy-start(f32[10,128,512]{2,1,0:T(8,128)} %get-tuple-element.19.slope) | copy-start | bytes 7864324
  24.2 19.6 %copy-start.2 = (bf16[10,128,512]{2,1,0:T(8,128)(2,1)S(1)}, bf16[10,128,512]{2,1,0:T(8,128)(2,1)}, u32[]{:S(2)}) copy-start(bf16[10,128,512]{2,1,0:T(8,128)(2,1)} %get-tuple-element.13.stack) | copy-start | bytes 3932164
  24.2 19.6 %copy-start.3 = (bf16[10,128,512]{2,1,0:T(8,128)(2,1)S(1)}, bf16[10,128,512]{2,1,0:T(8,128)(2,1)}, u32[]{:S(2)}) copy-start(bf16[10,128,512]{2,1,0:T(8,128)(2,1)} %get-tuple-element.18.agg) | copy-start | bytes 3932164
  24.2 19.6 %copy-start.4 = (f32[512]{0:T(512)S(1)}, f32[512]{0:T(512)}, u32[]{:S(2)}) copy-start(f32[512]{0:T(512)} %param.18) | copy-start | bytes 6148

commit v3 on v2

--- a/solution.py
+++ b/solution.py
@@ -111,7 +111,7 @@
         fetch.wait()
     token32 = token[...].astype(jnp.float32)
 
-    def aggregate(node_block, spot):
+    def aggregate(node_block):
         hidden = jnp.sum(
             jnp.where(rows == cols, mask[node_block].astype(jnp.float32), 0.0), axis=1, keepdims=True
         )
@@ -119,14 +119,30 @@
         mixed = jnp.dot(
             adj[node_block], masked32.astype(jnp.bfloat16), preferred_element_type=jnp.float32
         )
-        agg_out[spot] = (masked32 + mixed).astype(jnp.bfloat16)
+        return (masked32 + mixed).astype(jnp.bfloat16)
 
     for k in range(wanted):
-        aggregate(requests[served(t) * wanted + k], own_count + k)
+        asked[k] = aggregate(requests[served(t) * wanted + k])
+
+    def agg_copy(c):
+        return pltpu.make_async_remote_copy(
+            src_ref=asked.at[lax.rem(j + c, wanted)], dst_ref=landed.at[j],
+            send_sem=z_send.at[c], recv_sem=z_recv.at[c],
+            device_id=pair_of(c), device_id_type=MESH,
+        )
+
+    pl.when(jnp.logical_not(alone))(lambda: agg_copy(0).start())
+    for c in range(1, wanted):
+        agg_copy(c).start()
+
+    @pl.when(alone)
+    def _():
+        landed[j] = asked[j]
+
     across.wait_recv()
     relay.start()
     for k in range(own_count):
-        aggregate(t * own_count + k, k)
+        agg_out[k] = aggregate(t * own_count + k)
     near.wait_recv()
     relay.wait_recv()
 
@@ -138,36 +154,20 @@
         pre = jnp.dot(agg, matrix, preferred_element_type=jnp.float32) + shift
         sig = sigmoid(pre)
         slope_out[pl.ds(spot, many)] = (sig * (1.0 + pre * (1.0 - sig))).reshape(many, block, width)
-        return (pre * sig).astype(jnp.bfloat16).reshape(many, block, width)
-
-    for k in range(wanted):
-        asked[k] = activate(own_count + k, 1)[0]
-
-    def z_copy(c):
-        return pltpu.make_async_remote_copy(
-            src_ref=asked.at[lax.rem(j + c, wanted)], dst_ref=landed.at[j],
-            send_sem=z_send.at[c], recv_sem=z_recv.at[c],
-            device_id=pair_of(c), device_id_type=MESH,
-        )
-
-    pl.when(jnp.logical_not(alone))(lambda: z_copy(0).start())
-    for c in range(1, wanted):
-        z_copy(c).start()
-
-    @pl.when(alone)
-    def _():
-        landed[j] = asked[j]
+        z = (pre * sig).astype(jnp.bfloat16).reshape(many, block, width)
+        stack_out[pl.ds(spot, many)] = z
+        return z
 
     for k in range(0, own_count, 2):
         z = activate(k, 2)
-        stack_out[pl.ds(k, 2)] = z
         scaled_out[pl.ds(k, 2)] = (z.astype(jnp.float32) * gain[...][None]).astype(jnp.bfloat16)
 
-    pl.when(jnp.logical_not(alone))(lambda: z_copy(0).wait())
+    pl.when(jnp.logical_not(alone))(lambda: agg_copy(0).wait())
     for c in range(1, wanted):
-        z_copy(c).wait()
-    for k in range(wanted):
-        stack_out[own_count + k] = landed[k]
+        agg_copy(c).wait()
+    for k in range(0, wanted, 2):
+        agg_out[pl.ds(own_count + k, 2)] = landed[pl.ds(k, 2)]
+        activate(own_count + k, 2)
     across.wait_send()
     near.wait_send()
     relay.wait_send()
@@ -241,13 +241,10 @@
             second_acc[ib] += part_b
 
 
-def decode_kernel(first, second, count, words, stack, scaled, first_acc, second_out, back_out, second_acc):
-    own_count = scaled.shape[0]
+def decode_kernel(first, second, count, words, stack, scaled, first_acc, second_acc):
     first_acc[...] = jnp.zeros_like(first_acc)
     second_acc[...] = jnp.zeros_like(second_acc)
     run_pairs(first, second, count, words, stack, scaled, first_acc, second_acc)
-    second_out[...] = second_acc[:own_count]
-    back_out[...] = second_acc[own_count:].astype(jnp.bfloat16)
 
 
 def decode(first, second, count, words, stack, scaled):
@@ -256,13 +253,11 @@
     return pl.pallas_call(
         decode_kernel,
         in_specs=[smem()] * 3 + [vmem()] * 3,
-        out_specs=[vmem()] * 3,
+        out_specs=[vmem()] * 2,
         out_shape=(
             jax.ShapeDtypeStruct((own_count, block, width), jnp.float32),
-            jax.ShapeDtypeStruct((own_count, block, width), jnp.float32),
-            jax.ShapeDtypeStruct((total - own_count, block, width), jnp.bfloat16),
-        ),
-        scratch_shapes=[pltpu.VMEM((total, block, width), jnp.float32)],
+            jax.ShapeDtypeStruct((total, block, width), jnp.float32),
+        ),
         compiler_params=pltpu.CompilerParams(vmem_limit_bytes=VMEM_LIMIT),
         cost_estimate=pl.CostEstimate(
             flops=64 * 6 * block * block * width, bytes_accessed=8 << 20, transcendentals=0
@@ -271,10 +266,10 @@
 
 
 def reduce_kernel(
-    doms, own_count, wanted, first, second, back, stack, agg, slope, gain, weight_out, bias_out, gain_out,
-    part, home, dpre, recv_core, sum_core, recv_y, total, recv_dom, recv_small, full,
+    doms, own_count, total_count, first, second, stack, agg, slope, gain, weight_out, bias_out, gain_out,
+    part, dpre, recv_core, sum_core, recv_y, total, recv_dom, recv_small, full,
     core_send, core_recv, y_send, y_recv, dom_send, dom_recv, small_send, small_recv,
-    full_send, full_recv, home_send, home_recv,
+    full_send, full_recv,
 ):
     d = lax.axis_index("dom")
     t = lax.axis_index("tp")
@@ -295,43 +290,6 @@
             barrier, inc=1, device_id={"dom": lax.rem(d + o, doms)}, device_id_type=MESH
         )
 
-    a = lax.div(d, wanted)
-    j = lax.rem(d, wanted)
-
-    def pair_of(c):
-        return t * wanted + lax.rem(j - c + wanted, wanted), served(a)
-
-    alone = jnp.logical_and(a == t, served(t) == t)
-    for c in range(wanted):
-        target = pair_of(c)
-        source = served(t) * wanted + lax.rem(j + c, wanted), a
-
-        def greet():
-            pl.semaphore_signal(barrier, inc=1, device_id=target, device_id_type=MESH)
-            pl.semaphore_signal(barrier, inc=1, device_id=source, device_id_type=MESH)
-
-        if c == 0:
-            pl.when(jnp.logical_not(alone))(greet)
-        else:
-            greet()
-
-    pl.semaphore_wait(barrier, doms + 1 + 2 * wanted - jnp.where(alone, 2, 0))
-
-    def home_copy(c):
-        return pltpu.make_async_remote_copy(
-            src_ref=back.at[lax.rem(j - c + wanted, wanted)], dst_ref=home.at[j],
-            send_sem=home_send.at[c], recv_sem=home_recv.at[c],
-            device_id=pair_of(c), device_id_type=MESH,
-        )
-
-    pl.when(jnp.logical_not(alone))(lambda: home_copy(0).start())
-    for c in range(1, wanted):
-        home_copy(c).start()
-
-    @pl.when(alone)
-    def _():
-        home[j] = back[j]
-
     block = stack.shape[1]
     bias_sum = jnp.zeros((1, width), jnp.float32)
     gain_sum = jnp.zeros((1, width), jnp.float32)
@@ -341,36 +299,25 @@
         value = (gain[...] * value + second[k]) * slope[k]
         bias_sum += jnp.sum(value, axis=0, keepdims=True)
         dpre[pl.ds(k * block, block), :] = value.astype(jnp.bfloat16)
+    for k in range(own_count, total_count):
+        value = second[k] * slope[k]
+        bias_sum += jnp.sum(value, axis=0, keepdims=True)
+        dpre[pl.ds(k * block, block), :] = value.astype(jnp.bfloat16)
 
     lanes, _, quarter = part.shape
-
-    def product(start, many, c):
-        left = agg[pl.ds(start, many)].reshape(many * block, width)
-        right = dpre[pl.ds(start * block, many * block), pl.ds(c * quarter, 2 * quarter)]
-        return lax.dot_general(
-            left, right, (((0,), (0,)), ((), ())), preferred_element_type=jnp.float32
-        )
-
+    left = agg[...].reshape(total_count * block, width)
+    row = lax.broadcasted_iota(jnp.int32, (8, width), 0)
+    extra = jnp.where(row == 0, bias_sum, jnp.where(row == 1, gain_sum, 0.0))
     for c in range(0, lanes, 2):
-        both = product(0, own_count, c)
+        both = lax.dot_general(
+            left, dpre[:, pl.ds(c * quarter, 2 * quarter)], (((0,), (0,)), ((), ())),
+            preferred_element_type=jnp.float32,
+        )
         for k in range(2):
             part[c + k, :width, :] = both[:, k * quarter : (k + 1) * quarter]
-
-    pl.when(jnp.logical_not(alone))(lambda: home_copy(0).wait())
-    for c in range(1, wanted):
-        home_copy(c).wait()
-    for k in range(wanted):
-        value = home[k].astype(jnp.float32) * slope[own_count + k]
-        bias_sum += jnp.sum(value, axis=0, keepdims=True)
-        dpre[pl.ds((own_count + k) * block, block), :] = value.astype(jnp.bfloat16)
-    for c in range(0, lanes, 2):
-        both = product(own_count, wanted, c)
-        for k in range(2):
-            part[c + k, :width, :] += both[:, k * quarter : (k + 1) * quarter]
-    row = lax.broadcasted_iota(jnp.int32, (8, width), 0)
-    extra = jnp.where(row == 0, bias_sum, jnp.where(row == 1, gain_sum, 0.0))
     for c in range(lanes):
         part[c, pl.ds(width, 8), :] = extra[:, c * quarter : (c + 1) * quarter]
+    pl.semaphore_wait(barrier, doms + 1)
 
     def core_copy(h):
         return pltpu.make_async_remote_copy(
@@ -461,16 +408,16 @@
     weight_out[...] = full[...]
 
 
-def reduce_all(doms, lanes, first, second, back, stack, agg, slope, gain):
+def reduce_all(doms, lanes, first, second, stack, agg, slope, gain):
     own_count, block, width = first.shape
-    wanted = back.shape[0]
+    total_count = second.shape[0]
     quarter = width // lanes
     tall = width + 8
     rows = width // doms
     dma = pltpu.SemaphoreType.DMA
     return pl.pallas_call(
-        functools.partial(reduce_kernel, doms, own_count, wanted),
-        in_specs=[vmem()] * 7,
+        functools.partial(reduce_kernel, doms, own_count, total_count),
+        in_specs=[vmem()] * 6,
         out_specs=[vmem()] * 3,
         out_shape=(
             jax.ShapeDtypeStruct((width, quarter), jnp.float32),
@@ -479,8 +426,7 @@
         ),
         scratch_shapes=[
             pltpu.VMEM((lanes, tall, quarter), jnp.float32),
-            pltpu.VMEM((wanted, block, width), jnp.bfloat16),
-            pltpu.VMEM(((own_count + wanted) * block, width), jnp.bfloat16),
+            pltpu.VMEM((total_count * block, width), jnp.bfloat16),
             pltpu.VMEM((2, tall, quarter), jnp.float32),
             pltpu.VMEM((tall, quarter), jnp.float32),
             pltpu.VMEM((tall, quarter), jnp.float32),
@@ -490,12 +436,11 @@
             pltpu.VMEM((width, quarter), jnp.float32),
             dma((2,)), dma((2,)), dma, dma,
             dma((doms,)), dma((doms,)), dma((doms,)), dma((doms,)), dma((doms,)), dma((doms,)),
-            dma((wanted,)), dma((wanted,)),
         ],
         compiler_params=pltpu.CompilerParams(
             collective_id=1, has_side_effects=True, vmem_limit_bytes=VMEM_LIMIT
         ),
-    )(first, second, back, stack, agg, slope, gain)
+    )(first, second, stack, agg, slope, gain)
 
 
 def body(
@@ -517,10 +462,10 @@
         node_mask.reshape(nblocks, 1, block),
         mask_token.reshape(1, width), enc_weight, enc_bias.reshape(1, -1), gain_row,
     )
-    first, second, back = decode(
+    first, second = decode(
         pair_first[0, 0], pair_second[0, 0], pair_count.reshape(1), label_words[0, 0], stack, scaled
     )
-    weight_grad, bias_grad, gain_grad = reduce_all(doms, lanes, first, second, back, stack, agg, slope, gain_row)
+    weight_grad, bias_grad, gain_grad = reduce_all(doms, lanes, first, second, stack, agg, slope, gain_row)
     return weight_grad, bias_grad.reshape(-1), gain_grad.reshape(-1)
 
 

time: 89.2 us -> 71.7 us (0.80); the launches traced: 88.5 us -> 72.4 us
  Pallas kernels: 81.6 us -> 65.4 us
    pallas_call x1, Pallas kernels: 43 us -> 31.7 us  [reduce_all(): pl.pallas_call(functools.partial(reduce_kernel, doms, own_count, total_co...]
    pallas_call x1, Pallas kernels: 19.5 us -> 16.9 us  [decode(): pl.pallas_call(decode_kernel, in_specs=[smem()] * 3 + [vmem()] * 3, out_s...]
    pallas_call x1, Pallas kernels: 19.1 us -> 16.8 us  [front(): pl.pallas_call(functools.partial(front_kernel, own_count, wanted), in_spe...]
where the time goes in v3:
time: 71.7 us; the launch traced here: 72.4 us
  Pallas kernels  65.4 us (91%)
  local copies, waits for them, and re-layouts  5.55 us (8%)
  between operations  1.37 us (2%)
    pallas_call x1, Pallas kernels, reduce_all(): pl.pallas_call(functools.partial(reduce_kernel, doms, own_count, total_co...  31.7 us
    pallas_call x1, Pallas kernels, decode(): pl.pallas_call(decode_kernel, in_specs=[smem()] * 3 + [vmem()] * 3, out_s...  16.9 us
    pallas_call x1, Pallas kernels, front(): pl.pallas_call(functools.partial(front_kernel, own_count, wanted), in_spe...  16.8 us
    unnamed x21, local copies, waits for them, and re-layouts  4.29 us

profile of v3, /device:TPU:0, one launch (start us, length us, event | category | flops | bytes accessed | tf_op | source)
XLA Modules:
  0.0 72.4 jit_solution(3251621706738851462)
XLA Ops:
  1.3 1.3 %reshape.41.token_hbm = bf16[1,512]{1,0:T(2,128)(2,1)} reshape(bf16[512]{0:T(512)(128)(2,1)} %param.15) | data formatting | bytes 2048 | tf_op jit(solution)/shard_map/reshape | solution.py:463
  2.5 0.0 copy-start.6
  2.5 0.0 copy-start.7
  2.5 0.0 copy-start.8
  2.5 16.8 %shard_map.139 = (bf16[10,128,512]{2,1,0:T(8,128)(2,1)}, bf16[8,128,512]{2,1,0:T(8,128)(2,1)}, bf16[10,128,512]{2,1,0:T(8,128)(2,1)}, f32[10,128,512]{2,1,0:T(8,128)}) custom-call(s32[8]{0:T(128)} %bitcast.23, bf16[32,128,512]{2,1,0:T(8,128)(2,1)} %bitcast.20, bf16[32,128,128]{2,1,0:T(8,128)(2,1)} %bitcast.21, s32[32,1,128]{2,1,0:T(1,128)} %bitcast.22, ...), custom_call_target="tpu_custom_call" | custom-call | tf_op jit(solution)/shard_map/pallas_call | solution.py:182
  19.4 0.0 copy-done.6
  19.4 0.0 copy-done.7
  19.4 0.0 copy-done.8
  19.4 0.0 copy-start.1
  19.4 1.3 %copy-done.1 = bf16[10,128,512]{2,1,0:T(8,128)(2,1)S(1)} copy-done((bf16[10,128,512]{2,1,0:T(8,128)(2,1)S(1)}, bf16[10,128,512]{2,1,0:T(8,128)(2,1)}, u32[]{:S(2)}) %copy-start.1) | copy-done | bytes 1310744
  20.7 0.0 copy-start.5
  20.7 1.2 %copy-done.5 = bf16[8,128,512]{2,1,0:T(8,128)(2,1)S(1)} copy-done((bf16[8,128,512]{2,1,0:T(8,128)(2,1)S(1)}, bf16[8,128,512]{2,1,0:T(8,128)(2,1)}, u32[]{:S(2)}) %copy-start.5) | copy-done | bytes 1048600
  22.0 0.0 copy-start
  22.0 0.0 copy-start.2
  22.0 0.0 copy-start.3
  22.0 0.0 copy-start.4
  22.0 16.9 %shard_map.140 = (f32[8,128,512]{2,1,0:T(8,128)S(1)}, f32[10,128,512]{2,1,0:T(8,128)S(1)}) custom-call(s32[64]{0:T(128)S(1)} %bitcast.16, s32[64]{0:T(128)S(1)} %bitcast.17, s32[1]{0:T(128)} %bitcast.12.count, s32[64,8,128]{2,1,0:T(8,128)S(1)} %bitcast.15, bf16[10,128,512]{2,1,0:T(8,128)(2,1)S(1)} %copy-done.1, bf16[8,128,512]{2,1,0:T(8,128)(2,1)S(1)} %copy-done.5), custom_call_target="tpu_custom_call" | custom-call | flops 3221225472 | bytes 8388608 | tf_op jit(solution)/shard_map/pallas_call | solution.py:253
  38.9 0.0 copy-done
  38.9 0.0 copy-done.2
  38.9 0.0 copy-done.3
  38.9 0.0 copy-done.4
  38.9 31.7 %shard_map.141 = (f32[512,128]{1,0:T(8,128)S(1)}, f32[1,128]{1,0:T(1,128)S(1)}, f32[1,128]{1,0:T(1,128)S(1)}) custom-call(f32[8,128,512]{2,1,0:T(8,128)S(1)} %get-tuple-element.14.first, f32[10,128,512]{2,1,0:T(8,128)S(1)} %get-tuple-element.15.second, bf16[10,128,512]{2,1,0:T(8,128)(2,1)S(1)} %copy-done.2, bf16[10,128,512]{2,1,0:T(8,128)(2,1)S(1)} %copy-done.3, ...), custom_call_target="tpu_custom_call" | custom-call | tf_op jit(solution)/shard_map/pallas_call | solution.py:418
  70.6 0.7 copy.19
  71.3 0.5 copy.20
  71.8 0.5 copy.21
Async XLA Ops:
  2.5 16.9 %copy-start.6 = (s32[1,1,64,8,128]{4,3,2,1,0:T(8,128)S(1)}, s32[1,1,64,8,128]{4,3,2,1,0:T(8,128)}, u32[]{:S(2)}) copy-start(s32[1,1,64,8,128]{4,3,2,1,0:T(8,128)} %param.22) | copy-start | bytes 786436
  2.5 16.9 %copy-start.7 = (s32[1,1,64]{2,1,0:T(1,128)S(1)}, s32[1,1,64]{2,1,0:T(1,128)}, u32[]{:S(2)}) copy-start(s32[1,1,64]{2,1,0:T(1,128)} %param.20) | copy-start | bytes 772
  2.5 16.9 %copy-start.8 = (s32[1,1,64]{2,1,0:T(1,128)S(1)}, s32[1,1,64]{2,1,0:T(1,128)}, u32[]{:S(2)}) copy-start(s32[1,1,64]{2,1,0:T(1,128)} %param.21) | copy-start | bytes 772
  19.4 1.3 %copy-start.1 = (bf16[10,128,512]{2,1,0:T(8,128)(2,1)S(1)}, bf16[10,128,512]{2,1,0:T(8,128)(2,1)}, u32[]{:S(2)}) copy-start(bf16[10,128,512]{2,1,0:T(8,128)(2,1)} %get-tuple-element.12.stack) | copy-start | bytes 3932164
  20.7 1.2 %copy-start.5 = (bf16[8,128,512]{2,1,0:T(8,128)(2,1)S(1)}, bf16[8,128,512]{2,1,0:T(8,128)(2,1)}, u32[]{:S(2)}) copy-start(bf16[8,128,512]{2,1,0:T(8,128)(2,1)} %get-tuple-element.13.scaled) | copy-start | bytes 3145732
  22.0 16.9 %copy-start = (f32[10,128,512]{2,1,0:T(8,128)S(1)}, f32[10,128,512]{2,1,0:T(8,128)}, u32[]{:S(2)}) copy-start(f32[10,128,512]{2,1,0:T(8,128)} %get-tuple-element.17.slope) | copy-start | bytes 7864324
  22.0 16.9 %copy-start.2 = (bf16[10,128,512]{2,1,0:T(8,128)(2,1)S(1)}, bf16[10,128,512]{2,1,0:T(8,128)(2,1)}, u32[]{:S(2)}) copy-start(bf16[10,128,512]{2,1,0:T(8,128)(2,1)} %get-tuple-element.12.stack) | copy-start | bytes 3932164
  22.0 16.9 %copy-start.3 = (bf16[10,128,512]{2,1,0:T(8,128)(2,1)S(1)}, bf16[10,128,512]{2,1,0:T(8,128)(2,1)}, u32[]{:S(2)}) copy-start(bf16[10,128,512]{2,1,0:T(8,128)(2,1)} %get-tuple-element.16.agg) | copy-start | bytes 3932164
  22.0 17.0 %copy-start.4 = (f32[512]{0:T(512)S(1)}, f32[512]{0:T(512)}, u32[]{:S(2)}) copy-start(f32[512]{0:T(512)} %param.18) | copy-start | bytes 6148

commit v4 on v3

--- a/solution.py
+++ b/solution.py
@@ -7,7 +7,7 @@
 from jax.experimental.pallas import tpu as pltpu
 from jax.sharding import PartitionSpec as P
 
-UNROLL = 4
+UNROLL = 8
 INV_NORM = 1.0 / 256.0
 MESH = pl.DeviceIdType.MESH
 VMEM_LIMIT = 32 * 1024 * 1024

time: 71.7 us -> 70.8 us (0.987)
    pallas_call x1, Pallas kernels: 16.9 us -> 12.4 us  [decode(): pl.pallas_call(decode_kernel, in_specs=[smem()] * 3 + [vmem()] * 3, out_s...]
    pallas_call x1, Pallas kernels: 31.7 us -> 35.7 us  [reduce_all(): pl.pallas_call(functools.partial(reduce_kernel, doms, own_count, total_co...]
where the time goes in v4:
time: 70.8 us; the launch traced here: 71.9 us
  Pallas kernels  65 us (92%)
  local copies, waits for them, and re-layouts  5.55 us (8%)
  between operations  1.37 us (2%)
    pallas_call x1, Pallas kernels, reduce_all(): pl.pallas_call(functools.partial(reduce_kernel, doms, own_count, total_co...  35.7 us
    pallas_call x1, Pallas kernels, front(): pl.pallas_call(functools.partial(front_kernel, own_count, wanted), in_spe...  16.8 us
    pallas_call x1, Pallas kernels, decode(): pl.pallas_call(decode_kernel, in_specs=[smem()] * 3 + [vmem()] * 3, out_s...  12.4 us
    unnamed x21, local copies, waits for them, and re-layouts  4.29 us

profile of v4, /device:TPU:0, one launch (start us, length us, event | category | flops | bytes accessed | tf_op | source)
XLA Modules:
  0.0 71.9 jit_solution(615595400516436085)
XLA Ops:
  1.3 1.3 %reshape.41.token_hbm = bf16[1,512]{1,0:T(2,128)(2,1)} reshape(bf16[512]{0:T(512)(128)(2,1)} %param.15) | data formatting | bytes 2048 | tf_op jit(solution)/shard_map/reshape | solution.py:463
  2.5 0.0 copy-start.6
  2.5 0.0 copy-start.7
  2.5 0.0 copy-start.8
  2.5 16.8 %shard_map.139 = (bf16[10,128,512]{2,1,0:T(8,128)(2,1)}, bf16[8,128,512]{2,1,0:T(8,128)(2,1)}, bf16[10,128,512]{2,1,0:T(8,128)(2,1)}, f32[10,128,512]{2,1,0:T(8,128)}) custom-call(s32[8]{0:T(128)} %bitcast.23, bf16[32,128,512]{2,1,0:T(8,128)(2,1)} %bitcast.20, bf16[32,128,128]{2,1,0:T(8,128)(2,1)} %bitcast.21, s32[32,1,128]{2,1,0:T(1,128)} %bitcast.22, ...), custom_call_target="tpu_custom_call" | custom-call | tf_op jit(solution)/shard_map/pallas_call | solution.py:182
  19.4 0.0 copy-done.6
  19.4 0.0 copy-done.7
  19.4 0.0 copy-done.8
  19.4 0.0 copy-start.1
  19.4 1.3 %copy-done.1 = bf16[10,128,512]{2,1,0:T(8,128)(2,1)S(1)} copy-done((bf16[10,128,512]{2,1,0:T(8,128)(2,1)S(1)}, bf16[10,128,512]{2,1,0:T(8,128)(2,1)}, u32[]{:S(2)}) %copy-start.1) | copy-done | bytes 1310744
  20.7 0.0 copy-start.5
  20.7 1.2 %copy-done.5 = bf16[8,128,512]{2,1,0:T(8,128)(2,1)S(1)} copy-done((bf16[8,128,512]{2,1,0:T(8,128)(2,1)S(1)}, bf16[8,128,512]{2,1,0:T(8,128)(2,1)}, u32[]{:S(2)}) %copy-start.5) | copy-done | bytes 1048600
  22.0 0.0 copy-start
  22.0 0.0 copy-start.2
  22.0 0.0 copy-start.3
  22.0 0.0 copy-start.4
  22.0 12.4 %shard_map.140 = (f32[8,128,512]{2,1,0:T(8,128)S(1)}, f32[10,128,512]{2,1,0:T(8,128)S(1)}) custom-call(s32[64]{0:T(128)S(1)} %bitcast.16, s32[64]{0:T(128)S(1)} %bitcast.17, s32[1]{0:T(128)} %bitcast.12.count, s32[64,8,128]{2,1,0:T(8,128)S(1)} %bitcast.15, bf16[10,128,512]{2,1,0:T(8,128)(2,1)S(1)} %copy-done.1, bf16[8,128,512]{2,1,0:T(8,128)(2,1)S(1)} %copy-done.5), custom_call_target="tpu_custom_call" | custom-call | flops 3221225472 | bytes 8388608 | tf_op jit(solution)/shard_map/pallas_call | solution.py:253
  34.4 0.0 copy-done
  34.4 0.0 copy-done.2
  34.4 0.0 copy-done.3
  34.4 0.0 copy-done.4
  34.4 35.7 %shard_map.141 = (f32[512,128]{1,0:T(8,128)S(1)}, f32[1,128]{1,0:T(1,128)S(1)}, f32[1,128]{1,0:T(1,128)S(1)}) custom-call(f32[8,128,512]{2,1,0:T(8,128)S(1)} %get-tuple-element.14.first, f32[10,128,512]{2,1,0:T(8,128)S(1)} %get-tuple-element.15.second, bf16[10,128,512]{2,1,0:T(8,128)(2,1)S(1)} %copy-done.2, bf16[10,128,512]{2,1,0:T(8,128)(2,1)S(1)} %copy-done.3, ...), custom_call_target="tpu_custom_call" | custom-call | tf_op jit(solution)/shard_map/pallas_call | solution.py:418
  70.1 0.7 copy.19
  70.8 0.5 copy.20
  71.4 0.5 copy.21
Async XLA Ops:
  2.5 16.9 %copy-start.6 = (s32[1,1,64,8,128]{4,3,2,1,0:T(8,128)S(1)}, s32[1,1,64,8,128]{4,3,2,1,0:T(8,128)}, u32[]{:S(2)}) copy-start(s32[1,1,64,8,128]{4,3,2,1,0:T(8,128)} %param.22) | copy-start | bytes 786436
  2.5 16.9 %copy-start.7 = (s32[1,1,64]{2,1,0:T(1,128)S(1)}, s32[1,1,64]{2,1,0:T(1,128)}, u32[]{:S(2)}) copy-start(s32[1,1,64]{2,1,0:T(1,128)} %param.20) | copy-start | bytes 772
  2.5 16.9 %copy-start.8 = (s32[1,1,64]{2,1,0:T(1,128)S(1)}, s32[1,1,64]{2,1,0:T(1,128)}, u32[]{:S(2)}) copy-start(s32[1,1,64]{2,1,0:T(1,128)} %param.21) | copy-start | bytes 772
  19.4 1.3 %copy-start.1 = (bf16[10,128,512]{2,1,0:T(8,128)(2,1)S(1)}, bf16[10,128,512]{2,1,0:T(8,128)(2,1)}, u32[]{:S(2)}) copy-start(bf16[10,128,512]{2,1,0:T(8,128)(2,1)} %get-tuple-element.12.stack) | copy-start | bytes 3932164
  20.7 1.2 %copy-start.5 = (bf16[8,128,512]{2,1,0:T(8,128)(2,1)S(1)}, bf16[8,128,512]{2,1,0:T(8,128)(2,1)}, u32[]{:S(2)}) copy-start(bf16[8,128,512]{2,1,0:T(8,128)(2,1)} %get-tuple-element.13.scaled) | copy-start | bytes 3145732
  22.0 12.4 %copy-start = (f32[10,128,512]{2,1,0:T(8,128)S(1)}, f32[10,128,512]{2,1,0:T(8,128)}, u32[]{:S(2)}) copy-start(f32[10,128,512]{2,1,0:T(8,128)} %get-tuple-element.17.slope) | copy-start | bytes 7864324
  22.0 12.4 %copy-start.2 = (bf16[10,128,512]{2,1,0:T(8,128)(2,1)S(1)}, bf16[10,128,512]{2,1,0:T(8,128)(2,1)}, u32[]{:S(2)}) copy-start(bf16[10,128,512]{2,1,0:T(8,128)(2,1)} %get-tuple-element.12.stack) | copy-start | bytes 3932164
  22.0 12.4 %copy-start.3 = (bf16[10,128,512]{2,1,0:T(8,128)(2,1)S(1)}, bf16[10,128,512]{2,1,0:T(8,128)(2,1)}, u32[]{:S(2)}) copy-start(bf16[10,128,512]{2,1,0:T(8,128)(2,1)} %get-tuple-element.16.agg) | copy-start | bytes 3932164
  22.0 12.5 %copy-start.4 = (f32[512]{0:T(512)S(1)}, f32[512]{0:T(512)}, u32[]{:S(2)}) copy-start(f32[512]{0:T(512)} %param.18) | copy-start | bytes 6148
